TPU v7x, 512 devices: a whole 4x8x8 slice. The times are simulated.
512 devices in a mesh: seg: 64 (over y, x, core), head: 8 (over z).
Axes of the slice: x: 4, y: 8, z: 8, core: 2. Of those that a mesh axis runs over, the one named last changes fastest.
Arguments:
- head_input: bfloat16 [1536, 131072], P('head', 'seg'), may hold values from -6 to 6
- gate_input: bfloat16 [1536, 131072], P('head', 'seg'), may hold values from -8 to 8
- input_map: bfloat16 [131072, 128], P('seg'), may hold values from -6 to 6
- output_map: bfloat16 [131072, 128], P('seg'), may hold values from -0.5 to 0.5
- step_size: float32 [24, 131072], P('head', 'seg'), may hold values from 0 to 1
- log_decay: float32 [24, 131072], P('head', 'seg'), may hold values from -1 to 0
- skip_gain: float32 [24], P('head'), may hold values from 0.5 to 1.5
- residual: bfloat16 [1536, 131072], P('head', 'seg'), may hold values from -6 to 6
- boundary: int32 [131072], P('seg'), may hold values from 0 to 1, as said below
- norm_gain: bfloat16 [1536], P('head'), may hold values from 0.099609375 to 1.8984375
- out_weight: bfloat16 [1536, 1536], P('head'), may hold values from -0.15625 to 0.15625
Outputs:
- span_rows: bfloat16 [32768, 1536], P(('seg', 'head'))
Inputs may be any that keep to these rules, and one draw needn't show every extreme that they name: `boundary`: each segment of 2048 positions holds between 128 and 512 ones, exactly 512 in some segment.
All inputs are finite; a program needn't handle non-finite values.
Results may differ from a plain program's by a relative error of at most 0.015.
Values may be sent and summed in bfloat16 or wider, within the bound.
No kernel may reach another device: no remote copies, remote signals or barrier semaphores. Data moves between devices by JAX's collectives and lax.ppermute only.
A program may use at most 64 MiB of HBM per device.

v0:
```python
import jax
import jax.numpy as jnp
from jax import lax
from jax.sharding import PartitionSpec as P


def on_device(
    head_input,
    gate_input,
    input_map,
    output_map,
    step_size,
    log_decay,
    skip_gain,
    residual,
    boundary,
    norm_gain,
    out_weight,
):
    local_width = head_input.shape[0]
    length = head_input.shape[1]
    heads_here = step_size.shape[0]
    head_width = local_width // heads_here
    state_width = input_map.shape[1]
    full_width = out_weight.shape[1]
    block_size = min(512, length)
    block_count = length // block_size
    inputs_blocked = head_input.reshape(heads_here, head_width, block_count, block_size).transpose(
        2, 3, 0, 1
    )
    input_blocked = input_map.reshape(block_count, block_size, state_width)
    output_blocked = output_map.reshape(block_count, block_size, state_width)
    steps_blocked = step_size.reshape(heads_here, block_count, block_size).transpose(1, 0, 2)
    decay_blocked = log_decay.reshape(heads_here, block_count, block_size).transpose(1, 0, 2)
    lower = jnp.arange(block_size)[:, None] >= jnp.arange(block_size)[None, :]

    def advance(carry, item):
        x_block, in_block, out_block, step_block, decay_block = item
        running = jnp.cumsum(decay_block, axis=1)
        last = running[:, -1]
        scores = jnp.dot(out_block, in_block.T, preferred_element_type=jnp.float32)
        spread = running[:, :, None] - running[:, None, :]
        decay = jnp.where(lower[None], jnp.exp(jnp.where(lower[None], spread, 0.0)), 0.0)
        weights = (scores[None] * decay * step_block[:, None, :]).astype(jnp.bfloat16)
        inner = jnp.einsum("hts,shp->thp", weights, x_block, preferred_element_type=jnp.float32)
        factor = (step_block * jnp.exp(last[:, None] - running)).T
        scaled = (x_block * factor[:, :, None]).astype(jnp.bfloat16)
        added = jnp.einsum("shp,sn->hpn", scaled, in_block, preferred_element_type=jnp.float32)
        return (jnp.exp(last)[:, None, None] * carry + added, (carry, inner, running))

    start = jnp.zeros((heads_here, head_width, state_width), jnp.float32)
    final_state, (local_starts, inner_out, running_all) = lax.scan(
        advance,
        start,
        (inputs_blocked, input_blocked, output_blocked, steps_blocked, decay_blocked),
    )
    block_ends = running_all[:, :, -1]
    segment_log = jnp.sum(block_ends, axis=0)
    before_block = jnp.cumsum(block_ends, axis=0) - block_ends
    logs_all = lax.all_gather(segment_log[None, :], "seg", axis=0, tiled=True)
    my_index = lax.axis_index("seg")
    totals = jnp.cumsum(logs_all, axis=0)
    before_me = totals[my_index] - logs_all[my_index]
    earlier = jnp.arange(logs_all.shape[0])[:, None] < my_index
    gaps = jnp.where(earlier, before_me[None, :] - totals, 0.0)
    factors = jnp.where(earlier, jnp.exp(gaps), 0.0)
    incoming = start + jnp.einsum(
        "jh,jhpn->hpn",
        factors,
        lax.all_gather(final_state[None].astype(jnp.bfloat16), "seg", axis=0, tiled=True).astype(
            jnp.float32
        ),
        precision=lax.Precision.HIGHEST,
    )
    block_states = local_starts + jnp.exp(before_block)[:, :, None, None] * incoming[None]
    state_half = block_states.astype(jnp.bfloat16)
    outer = jnp.einsum(
        "bqn,bhpn->bqhp", output_blocked, state_half, preferred_element_type=jnp.float32
    )
    outer = outer * jnp.exp(running_all).transpose(0, 2, 1)[:, :, :, None]
    ssd_out = (
        inner_out + outer + skip_gain[None, None, :, None] * inputs_blocked.astype(jnp.float32)
    ).astype(jnp.bfloat16)
    ssd_out = ssd_out.reshape(length, local_width)
    capacity = length // 4
    running_flags = jnp.cumsum(boundary)
    count = running_flags[-1]
    slots = jnp.arange(capacity, dtype=jnp.int32)
    positions = jnp.sum((running_flags[None, :] <= slots[:, None]).astype(jnp.int32), axis=1)
    positions = jnp.minimum(positions, length - 1)
    y_rows = jnp.take(ssd_out, positions, axis=0)
    gate_rows = jnp.take(gate_input, positions, axis=1).T
    resid_rows = jnp.take(residual, positions, axis=1).T
    used = slots < count
    gated = y_rows.astype(jnp.float32) * jax.nn.silu(gate_rows.astype(jnp.float32))
    squares = lax.psum(jnp.sum(gated * gated, axis=1), "head")
    normed = (
        gated
        * lax.rsqrt(squares / full_width + 1e-05)[:, None]
        * norm_gain.astype(jnp.float32)[None, :]
    )
    normed = jnp.where(used[:, None], normed, 0.0).astype(jnp.bfloat16)
    resid_kept = jnp.where(used[:, None], resid_rows.astype(jnp.float32), 0.0)
    first_column = lax.axis_index("head") * local_width
    partial_out = jnp.dot(normed, out_weight, preferred_element_type=jnp.float32)
    own_columns = lax.dynamic_slice_in_dim(partial_out, first_column, local_width, 1) + resid_kept
    return lax.psum_scatter(
        lax.dynamic_update_slice_in_dim(partial_out, own_columns, first_column, 1).astype(
            jnp.bfloat16
        ),
        "head",
        scatter_dimension=0,
        tiled=True,
    )


def solution(mesh):
    return jax.shard_map(
        on_device,
        mesh=mesh,
        in_specs=(
            P("head", "seg"),
            P("head", "seg"),
            P("seg", None),
            P("seg", None),
            P("head", "seg"),
            P("head", "seg"),
            P("head"),
            P("head", "seg"),
            P("seg"),
            P("head"),
            P("head", None),
        ),
        out_specs=P(("seg", "head"), None),
        check_vma=False,
    )
```

profile of v0, /device:TPU:1, one launch (start us, length us, event | category | flops | bytes accessed | tf_op | source)
XLA Modules:
  0.0 265.5 jit_solution(14556507780590587624)
XLA Ops:
  6.6 2.4 reshape.170
  9.1 29.7 %while.18 = (s32[]{:T(128)}, f32[3,64,128]{2,1,0:T(8,128)S(1)}, f32[4,3,64,128]{3,2,1,0:T(8,128)}, f32[4,512,3,64]{1,3,2,0:T(8,128)}, f32[4,3,512]{2,1,0:T(4,128...) while((s32[]{:T(128)}, f32[3,64,128]{2,1,0:T(8,128)S(1)}, ...), condition=%wide.region_6.7_spmd.clone.clone, body=%wide.region_3.6_spmd.clone.clone.sunk | while | flops 198513200 | bytes 4358684 | solution.py:52
  12.2 1.2 fusion.61
  13.5 2.2 fusion.62
  19.6 1.2 fusion.61
  20.9 2.2 fusion.62
  28.3 2.2 fusion.62
  34.4 1.2 fusion.61
  35.7 2.2 fusion.62
  39.5 1.3 dynamic-slice
  41.9 130.5 %all-reduce = f32[192]{0:T(256)S(1)} all-reduce(f32[192]{0:T(256)S(1)} %dynamic-update-slice), channel_id=2, replica_groups=mesh['seg'=64,'head'=8] {'seg'}, use_global_device_ids=true, to_apply=%add | all-reduce | flops 192 | bytes 1536
  173.3 1.4 copy.31
  176.2 1.4 copy.32
  178.1 2.6 gather_fusion.1
  180.7 2.6 gather_fusion.2
  183.3 1.3 iota_compare_fusion.2
  184.7 4.6 %fusion.23 = f32[3,1,64,128]{3,1,2,0:T(1,128)S(1)} fusion(f32[64,3,1,1]{0,2,3,1:T(1,128)S(1)} %copy.33, bf16[64,3,64,128]{3,2,1,0:T(8,128)(2,1)} %bitcast.147), kind=kOutput, calls=%fused_computation.39 | convolution fusion | flops 18874368 | bytes 3244800 | tf_op jit(solution)/shard_map/jh,jhpn->hpn/dot_general | solution.py:67
  189.3 1.2 fusion.27
  191.9 2.0 gather_fusion
  194.3 14.8 %psum.7 = f32[512]{0:T(512)S(1)} all-reduce(f32[512]{0:T(512)S(1)} %multiply_reduce_fusion), channel_id=1, replica_groups=mesh['seg'=64,'head'=8] {'head'}, use_global_device_ids=true, to_apply=%region_11.13 | all-reduce | flops 512 | bytes 4096 | tf_op jit(solution)/shard_map/psum | solution.py:96
  209.9 1.7 copy-done.1
  211.9 3.5 %dynamic_update_slice.15 = f32[512,1536]{1,0:T(8,128)} dynamic-update-slice(f32[512,1536]{1,0:T(8,128)} %copy-done.1, f32[512,192]{1,0:T(8,128)S(1)} %bitcast_add_fusion, s32[]{:T(128)} %constant.54.clone.1, s32[]{:T(128)S(6)} %select_n.65) | dynamic-update-slice | bytes 786436 | tf_op jit(solution)/shard_map/dynamic_update_slice | solution.py:108
  215.4 3.2 %convert_element_type.66 = bf16[512,1536]{1,0:T(8,128)(2,1)} convert(f32[512,1536]{1,0:T(8,128)} %dynamic_update_slice.15) | non-fusion elementwise | flops 786432 | bytes 4718592 | tf_op jit(solution)/shard_map/convert_element_type | solution.py:108
  218.6 40.0 %reduce-scatter.2.cloned.1.call-done = bf16[64,1536]{1,0:T(8,128)(2,1)} async-done(((bf16[512,1536]{1,0:T(8,128)(2,1)}), bf16[64,1536]{1,0:T(8,128)(2,1)}) %reduce-scatter.2.cloned.1.call-update) | async-done | bytes 196624 | tf_op jit(solution)/shard_map/reduce_scatter | solution.py:107
  (135 shorter events, 24.3 us)
Async XLA Ops:
  6.5 202.6 %copy-start = (bf16[192,1536]{1,0:T(8,128)(2,1)S(1)}, bf16[192,1536]{1,0:T(8,128)(2,1)}, u32[]{:S(2)}) copy-start(bf16[192,1536]{1,0:T(8,128)(2,1)} %param.25) | copy-start | bytes 1769476
  6.5 2.6 copy-start.2
  6.5 178.1 %all-gather.4.cloned.1.call-start = ((), (), s32[]{:S(2)}) async-start(), calls=%async_computation.2 | async-start | bytes 3194880 | tf_op jit(solution)/shard_map/all_gather | solution.py:70
  9.1 163.7 %copy-start.8 = (s32[2048]{0:T(1024)S(1)}, s32[2048]{0:T(1024)}, u32[]{:S(2)}) copy-start(s32[2048]{0:T(1024)} %param.23) | copy-start | bytes 24580
  9.1 166.4 %copy-start.10 = (bf16[192]{0:T(256)(128)(2,1)S(1)}, bf16[192]{0:T(256)(128)(2,1)}, u32[]{:S(2)}) copy-start(bf16[192]{0:T(256)(128)(2,1)} %param.24) | copy-start | bytes 1156
  39.5 219.2 %reduce-scatter.2.cloned.1.call-start = ((), (), s32[]{:S(2)}) async-start(), calls=%async_computation.1 | async-start | bytes 1769472 | tf_op jit(solution)/shard_map/reduce_scatter | solution.py:107
  180.7 8.6 %copy-start.3 = (bf16[4,512,128]{2,1,0:T(8,128)(2,1)S(1)}, bf16[4,512,128]{2,1,0:T(8,128)(2,1)}, u32[]{:S(2)}) copy-start(bf16[4,512,128]{2,1,0:T(8,128)(2,1)} %get-tuple-element.269) | copy-start | bytes 1572868
  183.3 6.0 %copy-start.4 = (f32[4,512,3,64]{1,3,2,0:T(8,128)S(1)}, f32[4,512,3,64]{1,3,2,0:T(8,128)}, u32[]{:S(2)}) copy-start(f32[4,512,3,64]{1,3,2,0:T(8,128)} %get-tuple-element.69) | copy-start | bytes 4718596
  184.7 4.6 %copy-start.7 = (f32[4,3,64,128]{3,2,1,0:T(8,128)S(1)}, f32[4,3,64,128]{3,2,1,0:T(8,128)}, u32[]{:S(2)}) copy-start(f32[4,3,64,128]{3,2,1,0:T(8,128)} %get-tuple-element.70) | copy-start | bytes 1179652
  191.2 2.7 %copy-start.5 = (bf16[512,192]{1,0:T(8,128)(2,1)S(1)}, bf16[512,192]{1,0:T(8,128)(2,1)}, u32[]{:S(2)}) copy-start(bf16[512,192]{1,0:T(8,128)(2,1)} %gather_fusion.1) | copy-start | bytes 589828
  191.2 17.9 %copy-start.9 = (pred[512]{0:T(512)(128)(4,1)S(1)}, pred[512]{0:T(512)(128)(4,1)}, u32[]{:S(2)}) copy-start(pred[512]{0:T(512)(128)(4,1)} %iota_compare_fusion.2) | copy-start | bytes 1540
  191.2 17.9 %copy-start.11 = (f32[192]{0:T(256)S(1)}, f32[192]{0:T(256)}, u32[]{:S(2)}) copy-start(f32[192]{0:T(256)} %convert_element_type.63) | copy-start | bytes 2308
  193.9 17.6 %copy-start.6 = (bf16[512,192]{1,0:T(8,128)(2,1)S(1)}, bf16[512,192]{1,0:T(8,128)(2,1)}, u32[]{:S(2)}) copy-start(bf16[512,192]{1,0:T(8,128)(2,1)} %gather_fusion.2) | copy-start | bytes 589828
  209.9 1.7 copy-start.1
Sparse Core Ops, SparseCore 0:
  39.6 89.1 all-gather.3
  218.7 39.8 reduce-scatter.1
where the time goes:
time: 269 us; the launch traced here: 265 us
  blocking collectives  145 us (54%)
  waiting for transfers between devices  40.1 us (15%)
  local copies, waits for them, and re-layouts  26 us (10%)
  matrix products  20.8 us (8%)
  other arithmetic  18.8 us (7%)
  between operations  14.3 us (5%)
    unnamed x1, blocking collectives  131 us
    reduce_scatter x1, waiting for transfers between devices, on_device(): lax.psum_scatter(lax.dynamic_update_slice_in_dim(partial_out, own_columns...  40 us
    psum x1, blocking collectives, on_device(): squares = lax.psum(jnp.sum(gated * gated, axis=1), 'head')  14.8 us
    dot_general x4, matrix products, advance(): jnp.einsum('hts,shp->thp', weights, x_block, preferred_element_type=jnp.f...  8.63 us
    unnamed x30, local copies, waits for them, and re-layouts  6.28 us
  transfers between devices with their start and end apart: 2, of which 1 were waited for; matrix products, arithmetic and copies ran while one was open for 5% of the time, Pallas kernels for 0%

commit v1 on v0

v1 whole, which is shorter than its diff:
```python
import functools

import jax
import jax.numpy as jnp
from jax import lax
from jax.experimental import pallas as pl
from jax.experimental.pallas import tpu as pltpu
from jax.sharding import Mesh
from jax.sharding import PartitionSpec as P

F32 = jnp.float32
BF16 = jnp.bfloat16
Q = 128
NT = (((1,), (1,)), ((), ()))
NN = (((1,), (0,)), ((), ()))


def dot(a, b, dims=NN):
    return lax.dot_general(a, b, dims, preferred_element_type=F32)


def pieces(v):
    hi = v.astype(BF16)
    rest = v - hi.astype(F32)
    mid = rest.astype(BF16)
    low = (rest - mid.astype(F32)).astype(BF16)
    return hi, mid, low


def dot3(v, b, dims=NN):
    return sum(dot(p, b, dims) for p in pieces(v))


def dot3r(a, v, dims=NT):
    return sum(dot(a, p, dims) for p in pieces(v))


def below(shape, strict=False):
    i = lax.broadcasted_iota(jnp.int32, shape, 0)
    j = lax.broadcasted_iota(jnp.int32, shape, 1)
    return jnp.where((i < j) if strict else (i <= j), 1.0, 0.0).astype(BF16)


def chunk_rows(ref, heads):
    n = ref.shape[1] // Q
    return jnp.concatenate([ref[:, c * Q : (c + 1) * Q] for c in range(n)], axis=0)


def log_tile(total, rows):
    heads = total.shape[0]
    lane = lax.broadcasted_iota(jnp.int32, (heads, Q), 1)
    hi, mid, low = pieces(jnp.broadcast_to(total, (heads, Q)))
    tile = jnp.where(
        lane == 0,
        hi.astype(F32),
        jnp.where(lane == 1, mid.astype(F32), jnp.where(lane == 2, low.astype(F32), 0.0)),
    )
    return jnp.concatenate([tile, jnp.zeros((rows - heads, Q), F32)], axis=0)


def final_state_kernel(heads, parts, x_ref, in_ref, step_ref, decay_ref, out_ref, scaled):
    width = x_ref.shape[0] // heads
    length = x_ref.shape[1]
    chunks = length // Q
    rows = width // parts
    logs = chunk_rows(decay_ref, heads)
    after = lax.broadcasted_iota(jnp.int32, (Q, Q), 0) > lax.broadcasted_iota(
        jnp.int32, (Q, Q), 1
    )
    suffix = dot3(logs, jnp.where(after, 1.0, 0.0).astype(BF16))
    sums = jnp.sum(logs, axis=1, keepdims=True)
    later = jnp.zeros((heads, 1), F32)
    for c in reversed(range(chunks)):
        here = slice(c * heads, (c + 1) * heads)
        lanes = slice(c * Q, (c + 1) * Q)
        factor = step_ref[:, lanes] * jnp.exp(suffix[here] + later)
        for h in range(heads):
            part = slice(h * width, (h + 1) * width)
            scaled[part, lanes] = (x_ref[part, lanes].astype(F32) * factor[h : h + 1]).astype(BF16)
        later = later + sums[here]
    state = dot(scaled[...], in_ref[...])
    tail = log_tile(later, out_ref.shape[1] - heads * rows)
    for j in range(parts):
        own = [state[h * width + j * rows : h * width + (j + 1) * rows] for h in range(heads)]
        out_ref[j] = jnp.concatenate(own + [tail], axis=0).astype(BF16)


def read_logs(block, heads, start):
    sums = jnp.sum(block[start:].astype(F32), axis=1, keepdims=True)
    return sums[:heads]


def spread(column, rows):
    return jnp.concatenate(
        [jnp.broadcast_to(column[h : h + 1], (rows, Q)) for h in range(column.shape[0])], axis=0
    )


def group_scan_kernel(heads, in_ref, before_ref, factor_ref, total_ref):
    parts = in_ref.shape[0]
    used = before_ref.shape[1]
    rows = used // heads
    state = jnp.zeros((used, Q), F32)
    log = jnp.zeros((heads, 1), F32)
    for i in range(parts):
        block = in_ref[i].astype(F32)
        before_ref[i] = state
        factor_ref[i] = spread(jnp.exp(log), rows)
        own = read_logs(block, heads, used)
        state = spread(jnp.exp(own), rows) * state + block[:used]
        log = log + own
    tail = log_tile(log, in_ref.shape[1] - used)
    whole = jnp.concatenate([state, tail], axis=0).astype(BF16)
    for j in range(total_ref.shape[0]):
        total_ref[j] = whole


def combine_kernel(heads, in_ref, before_ref, factor_ref, out_ref):
    used = before_ref.shape[1]
    rows = used // heads
    me = lax.axis_index("y")
    state = jnp.zeros((used, Q), F32)
    for g in range(in_ref.shape[0] - 1):
        block = in_ref[g].astype(F32)
        moved = spread(jnp.exp(read_logs(block, heads, used)), rows) * state + block[:used]
        state = jnp.where(g < me, moved, state)
    for i in range(before_ref.shape[0]):
        out_ref[i] = (before_ref[i] + factor_ref[i] * state).astype(BF16)


def local_kernel(
    heads,
    skip_ref,
    x_ref,
    gate_ref,
    res_ref,
    in_ref,
    out_map_ref,
    step_ref,
    decay_ref,
    flag_ref,
    value_ref,
    factor_ref,
    rows_ref,
    picked_ref,
    y_all,
    cums,
    pick,
):
    width = x_ref.shape[0] // heads
    length = x_ref.shape[1]
    chunks = length // Q
    upto = below((Q, Q))
    row = lax.broadcasted_iota(jnp.int32, (Q, Q), 0)
    col = lax.broadcasted_iota(jnp.int32, (Q, Q), 1)
    mask = row <= col
    eye = jnp.where(row == col, 1.0, 0.0).astype(BF16)
    down = jnp.where(col <= row, 1.0, 0.0).astype(BF16)
    logs = chunk_rows(decay_ref, heads)
    steps = chunk_rows(step_ref, heads)
    run_row = dot3(logs, upto)
    run_col = dot3r(down, logs)
    step_col = dot3r(eye, steps)
    state = [jnp.zeros((width, Q), F32) for _ in range(heads)]
    before = [jnp.zeros((1, 1), F32) for _ in range(heads)]
    for c in range(chunks):
        lanes = slice(c * Q, (c + 1) * Q)
        b = in_ref[lanes, :]
        o = out_map_ref[lanes, :]
        scores = dot(b, o, NT)
        for h in range(heads):
            k = c * heads + h
            part = slice(h * width, (h + 1) * width)
            run = run_row[k : k + 1]
            last = run[:, Q - 1 : Q]
            spread_log = run - run_col[:, k : k + 1]
            decay = jnp.where(mask, jnp.exp(spread_log), 0.0)
            weights = (scores * decay * step_col[:, k : k + 1]).astype(BF16)
            x = x_ref[part, lanes]
            xf = x.astype(F32)
            y = dot(x, weights) + skip_ref[h] * xf
            y = y + dot(state[h].astype(BF16), o, NT) * jnp.exp(run)
            y_all[part, lanes] = y.astype(BF16)
            scaled = (xf * (steps[k : k + 1] * jnp.exp(last - run))).astype(BF16)
            state[h] = jnp.exp(last) * state[h] + dot(scaled, b)
            for i, piece in enumerate(pieces(run + before[h])):
                cums[i * 8 + h : i * 8 + h + 1, lanes] = piece.astype(F32)
            before[h] = before[h] + last

    flags = flag_ref[...].astype(F32)
    within = dot(flags.astype(BF16), upto)
    rows = lax.broadcasted_iota(jnp.int32, (chunks, chunks), 0)
    cols = lax.broadcasted_iota(jnp.int32, (chunks, chunks), 1)
    sums = jnp.broadcast_to(within[:, Q - 1 : Q], (chunks, Q)).astype(BF16)
    earlier = dot(jnp.where(cols < rows, 1.0, 0.0).astype(BF16), sums)
    rank = jnp.where(flags > 0.0, within + earlier, 0.0) - 1.0
    slots = value_ref.shape[0]
    tile = 128
    slot = lax.broadcasted_iota(jnp.int32, (tile, Q), 0).astype(F32)
    for g in range(slots // tile):
        for c in range(chunks):
            hit = (rank[c : c + 1] - float(g * tile)) == slot
            pick[g * tile : (g + 1) * tile, c * Q : (c + 1) * Q] = jnp.where(hit, 1.0, 0.0).astype(
                BF16
            )
    log_pieces = cums[...].astype(BF16)
    for g in range(slots // tile):
        these = slice(g * tile, (g + 1) * tile)
        chosen = pick[these]
        gate = dot(chosen, gate_ref[...], NT)
        silu = gate / (1.0 + jnp.exp(-gate))
        value_ref[these] = dot(chosen, y_all[...], NT) * silu
        logs_at = dot(chosen, log_pieces, NT)
        for h in range(heads):
            run = logs_at[:, h : h + 1] + logs_at[:, 8 + h : 9 + h] + logs_at[:, 16 + h : 17 + h]
            part = slice(h * width, (h + 1) * width)
            factor_ref[these, part] = jnp.exp(run) * silu[:, part]
        rows_ref[these] = dot(chosen, out_map_ref[...]).astype(BF16)
        per = picked_ref.shape[1]
        taken = dot(chosen, res_ref[...], NT).astype(BF16)
        step = min(per, tile)
        for j in range(0, tile, step):
            to, at = divmod(g * tile + j, per)
            picked_ref[to, at : at + step] = taken[j : j + step]


def gate_kernel(heads, in_ref, rows_ref, value_ref, factor_ref, gain_ref, out_ref):
    parts = in_ref.shape[0]
    rows = in_ref.shape[1] // heads
    per = out_ref.shape[1]
    columns = value_ref.shape[1]
    held = in_ref[...].astype(F32)
    states = [held[:, h * rows : (h + 1) * rows].reshape(parts * rows, Q) for h in range(heads)]
    incoming = jnp.concatenate(states, axis=0).astype(BF16)
    outer = dot(rows_ref[...], incoming, NT)
    gated = value_ref[...] + factor_ref[...] * outer
    squares = jnp.sum(gated * gated, axis=1, keepdims=True)
    scaled = (gated * gain_ref[...].astype(F32)).astype(BF16)
    slots = gated.shape[0]
    pad = out_ref.shape[2] - columns
    lane = lax.broadcasted_iota(jnp.int32, (slots, pad), 1)
    hi, mid, low = pieces(jnp.broadcast_to(squares, (slots, pad)))
    extra = jnp.where(
        lane == 0,
        hi.astype(F32),
        jnp.where(lane == 1, mid.astype(F32), jnp.where(lane == 2, low.astype(F32), 0.0)),
    ).astype(BF16)
    for j in range(slots // per):
        these = slice(j * per, (j + 1) * per)
        out_ref[j, :, :columns] = scaled[these]
        out_ref[j, :, columns:] = extra[these]


def project_kernel(full_width, in_ref, res_ref, weight_ref, out_ref, lhs, res):
    groups, per, _ = in_ref.shape
    columns = res_ref.shape[2]
    halves = weight_ref.shape[0]
    half = weight_ref.shape[2]
    squares = jnp.zeros((per, 1), F32)
    for z in range(groups):
        block = in_ref[z]
        lhs[:, z * columns : (z + 1) * columns] = block[:, :columns]
        res[:, z * columns : (z + 1) * columns] = res_ref[z]
        squares = squares + jnp.sum(block[:, columns:].astype(F32), axis=1, keepdims=True)
    scale = lax.rsqrt(squares / full_width + 1e-05)
    for k in range(halves):
        part = slice(k * half, (k + 1) * half)
        done = dot(lhs[...], weight_ref[k])
        out_ref[:, part] = (done * scale + res[:, part].astype(F32)).astype(BF16)


def call(kernel, outs, args, scratch=(), smem=0, name=None):
    vmem = pl.BlockSpec(memory_space=pltpu.VMEM)
    specs = [pl.BlockSpec(memory_space=pltpu.SMEM)] * smem + [vmem] * (len(args) - smem)
    many = isinstance(outs, (tuple, list))
    return pl.pallas_call(
        kernel,
        out_shape=outs,
        in_specs=specs,
        out_specs=[vmem] * len(outs) if many else vmem,
        scratch_shapes=list(scratch),
        name=name,
    )(*args)


def on_device(
    head_input,
    gate_input,
    input_map,
    output_map,
    step_size,
    log_decay,
    skip_gain,
    residual,
    boundary,
    norm_gain,
    out_weight,
):
    S = jax.ShapeDtypeStruct
    group = ("x", "core")
    parts = lax.axis_size(group)
    groups = lax.axis_size("y")
    shares = lax.axis_size("head")
    local_width, length = head_input.shape
    heads = step_size.shape[0]
    full_width = out_weight.shape[1]
    slots = length // 4
    per = slots // shares
    used = local_width // parts
    height = used + 8

    half = full_width // lax.axis_size("core")
    own = lax.dynamic_slice_in_dim(out_weight, lax.axis_index("core") * half, half, 1)
    weight = lax.all_gather(own[None], ("core", "head"), axis=0, tiled=True)
    weight = weight.reshape(lax.axis_size("core"), shares * local_width, half)

    state = call(
        functools.partial(final_state_kernel, heads, parts),
        S((parts, height, Q), BF16),
        (head_input, input_map, step_size, log_decay),
        [pltpu.VMEM((local_width, length), BF16)],
        name="final_state",
    )
    moved = lax.all_to_all(state, group, 0, 0, tiled=True)
    before, factor, total = call(
        functools.partial(group_scan_kernel, heads),
        (
            S((parts, used, Q), F32),
            S((parts, used, Q), F32),
            S((groups, height, Q), BF16),
        ),
        (moved,),
        name="group_scan",
    )
    totals = lax.all_to_all(total, "y", 0, 0, tiled=True)
    value, decay, rows, picked = call(
        functools.partial(local_kernel, heads),
        (
            S((slots, local_width), F32),
            S((slots, local_width), F32),
            S((slots, Q), BF16),
            S((shares, per, local_width), BF16),
        ),
        (
            skip_gain,
            head_input,
            gate_input,
            residual,
            input_map,
            output_map,
            step_size,
            log_decay,
            boundary.reshape(length // Q, Q),
        ),
        [
            pltpu.VMEM((local_width, length), BF16),
            pltpu.VMEM((24, length), F32),
            pltpu.VMEM((slots, length), BF16),
        ],
        smem=1,
        name="local_ssd",
    )
    incoming = call(
        functools.partial(combine_kernel, heads),
        S((parts, used, Q), BF16),
        (totals, before, factor),
        name="combine",
    )
    kept = lax.all_to_all(picked, "head", 0, 0, tiled=True)
    incoming = lax.all_to_all(incoming, group, 0, 0, tiled=True)
    gated = call(
        functools.partial(gate_kernel, heads),
        S((shares, per, -(-(local_width + 3) // Q) * Q), BF16),
        (incoming, rows, value, decay, norm_gain.reshape(1, local_width)),
        name="gated",
    )
    gathered = lax.all_to_all(gated, "head", 0, 0, tiled=True)
    return call(
        functools.partial(project_kernel, full_width),
        S((per, full_width), BF16),
        (gathered, kept, weight),
        [pltpu.VMEM((per, full_width), BF16), pltpu.VMEM((per, full_width), BF16)],
        name="project",
    )


def solution(mesh):
    heads = mesh.shape["head"]
    segs = mesh.shape["seg"]
    core, x = (2, 4) if segs % 8 == 0 else (1, 1)
    if segs == 8:
        x = 2
    fine = Mesh(mesh.devices.reshape(segs // (x * core), x, core, heads), ("y", "x", "core", "head"))
    seg = ("y", "x", "core")
    return jax.shard_map(
        on_device,
        mesh=fine,
        in_specs=(
            P("head", seg),
            P("head", seg),
            P(seg, None),
            P(seg, None),
            P("head", seg),
            P("head", seg),
            P("head"),
            P("head", seg),
            P(seg),
            P("head"),
            P("head", None),
        ),
        out_specs=P((*seg, "head"), None),
        check_vma=False,
    )
```

time: 269 us -> 106 us (0.39); the launches traced: 265 us -> 105 us
  blocking collectives: 145 us -> 42.7 us
  waiting for transfers between devices: 40.1 us -> 9.35 us
  Pallas kernels: 0 us -> 23.9 us
  local copies, waits for them, and re-layouts: 26 us -> 2.39 us
  matrix products: 20.8 us -> 0 us
  other arithmetic: 18.8 us -> 0 us
  starting transfers between devices: 0.04 us -> 13.6 us
    unnamed x1 -> x0, blocking collectives: 131 us -> none
    all_to_all x0 -> x3, blocking collectives: none -> 42.7 us  [the longest x1 15.9 us: on_device(): gathered = lax.all_to_all(gated, 'head', 0, 0, tiled=True)]
    reduce_scatter x1 -> x0, waiting for transfers between devices: 40 us -> none  [on_device(): lax.psum_scatter(lax.dynamic_update_slice_in_dim(partial_out, own_columns...]
    pallas_call x0 -> x6, Pallas kernels: none -> 23.9 us  [call(): pl.pallas_call(kernel, out_shape=outs, in_specs=specs, out_specs=[vmem] *...]
    dot_general x15 -> x0, matrix products: 20.8 us -> none  [the longest x4 8.63 us: advance(): jnp.einsum('hts,shp->thp', weights, x_block, preferred_element_type=jnp.f...]
    psum x1 -> x0, blocking collectives: 14.8 us -> none  [on_device(): squares = lax.psum(jnp.sum(gated * gated, axis=1), 'head')]
    all_to_all x0 -> x2, starting transfers between devices: none -> 13.6 us  [the longest x1 8.45 us: on_device(): kept = lax.all_to_all(picked, 'head', 0, 0, tiled=True)]
    all_to_all x0 -> x2, waiting for transfers between devices: none -> 9.34 us  [the longest x1 9.33 us: on_device(): kept = lax.all_to_all(picked, 'head', 0, 0, tiled=True)]
  transfers between devices with their start and end apart: 2 -> 3, of which waited for: 1 -> 1; matrix products, arithmetic and copies ran while one was open for 5% -> 1% of each run, Pallas kernels for 0% -> 19%
where the time goes in v1:
time: 106 us; the launch traced here: 105 us
  blocking collectives  42.7 us (40%)
  Pallas kernels  23.9 us (23%)
  starting transfers between devices  13.6 us (13%)
  between operations  13.4 us (13%)
  waiting for transfers between devices  9.35 us (9%)
  local copies, waits for them, and re-layouts  2.39 us (2%)
    pallas_call x6, Pallas kernels, call(): pl.pallas_call(kernel, out_shape=outs, in_specs=specs, out_specs=[vmem] *...  23.9 us
    all_to_all x1, blocking collectives, on_device(): gathered = lax.all_to_all(gated, 'head', 0, 0, tiled=True)  15.9 us
    all_to_all x1, blocking collectives, on_device(): moved = lax.all_to_all(state, group, 0, 0, tiled=True)  15.6 us
    all_to_all x1, blocking collectives, on_device(): totals = lax.all_to_all(total, 'y', 0, 0, tiled=True)  11.3 us
    all_to_all x1, waiting for transfers between devices, on_device(): kept = lax.all_to_all(picked, 'head', 0, 0, tiled=True)  9.33 us
    all_to_all x1, starting transfers between devices, on_device(): kept = lax.all_to_all(picked, 'head', 0, 0, tiled=True)  8.45 us
    all_to_all x1, starting transfers between devices, on_device(): incoming = lax.all_to_all(incoming, group, 0, 0, tiled=True)  5.1 us
  transfers between devices with their start and end apart: 3, of which 1 were waited for; matrix products, arithmetic and copies ran while one was open for 1% of the time, Pallas kernels for 19%

profile of v1, /device:TPU:1, one launch (start us, length us, event | category | flops | bytes accessed | tf_op | source)
XLA Modules:
  0.0 105.4 jit_solution(5091298592747874694)
XLA Ops:
  6.5 0.0 copy-start
  6.5 0.0 copy-start.3
  6.5 0.0 all-gather.3.cloned.1.call-start
  6.5 1.1 %copy-done = bf16[192,1536]{1,0:T(8,128)(2,1)S(1)} copy-done((bf16[192,1536]{1,0:T(8,128)(2,1)S(1)}, bf16[192,1536]{1,0:T(8,128)(2,1)}, u32[]{:S(2)}) %copy-start) | copy-done | bytes 589848
  7.6 0.7 constant_dynamic-slice_fusion
  8.3 0.0 all-gather.3.cloned.1.call-update
  8.4 2.5 %final_state.1 = bf16[8,32,128]{2,1,0:T(8,128)(2,1)} custom-call(bf16[192,2048]{1,0:T(8,128)(2,1)} %x_ref.3, bf16[2048,128]{1,0:T(8,128)(2,1)} %in_ref.3, f32[3,2048]{1,0:T(4,128)} %step_ref.3, f32[3,2048]{1,0:T(4,128)} %decay_ref.3), custom_call_target="tpu_custom_call" | custom-call | tf_op jit(solution)/shard_map/final_state/pallas_call | solution.py:276
  10.9 15.6 %all_to_all.25.in_ref = bf16[8,32,128]{2,1,0:T(8,128)(2,1)} all-to-all(bf16[8,32,128]{2,1,0:T(8,128)(2,1)} %final_state.1), channel_id=1, replica_groups=mesh['y'=8,'x'=4,'core'=2,'head'=8] {'x','core'}, dimensions={0} | all-to-all | bytes 131072 | tf_op jit(solution)/shard_map/all_to_all | solution.py:324
  26.5 1.6 %group_scan.1 = (f32[8,24,128]{2,1,0:T(8,128)}, f32[8,24,128]{2,1,0:T(8,128)}, bf16[8,32,128]{2,1,0:T(8,128)(2,1)}) custom-call(bf16[8,32,128]{2,1,0:T(8,128)(2,1)} %all_to_all.25.in_ref), custom_call_target="tpu_custom_call" | custom-call | tf_op jit(solution)/shard_map/group_scan/pallas_call | solution.py:276
  28.2 11.3 %all_to_all.26.in_ref = bf16[8,32,128]{2,1,0:T(8,128)(2,1)} all-to-all(bf16[8,32,128]{2,1,0:T(8,128)(2,1)} %get-tuple-element.12), channel_id=1, replica_groups=mesh['y'=8,'x'=4,'core'=2,'head'=8] {'y'}, dimensions={0} | all-to-all | bytes 131072 | tf_op jit(solution)/shard_map/all_to_all | solution.py:335
  39.4 1.7 %combine.1 = bf16[8,24,128]{2,1,0:T(8,128)(2,1)} custom-call(bf16[8,32,128]{2,1,0:T(8,128)(2,1)} %all_to_all.26.in_ref, f32[8,24,128]{2,1,0:T(8,128)} %get-tuple-element.13.before_ref, f32[8,24,128]{2,1,0:T(8,128)} %get-tuple-element.14.factor_ref), custom_call_target="tpu_custom_call" | custom-call | tf_op jit(solution)/shard_map/combine/pallas_call | solution.py:276
  41.1 5.1 %all-to-all-start.2 = ((bf16[8,24,128]{2,1,0:T(8,128)(2,1)}), bf16[8,24,128]{2,1,0:T(8,128)(2,1)S(1)}, u32[]{:S(2)}, u32[]{:S(2)}) async-start(bf16[8,24,128]{2,1,0:T(8,128)(2,1)} %combine.1), calls=%async_computation.2 | async-start | bytes 98304 | tf_op jit(solution)/shard_map/all_to_all | solution.py:370
  46.2 11.4 %local_ssd.1 = (f32[512,192]{1,0:T(8,128)}, f32[512,192]{1,0:T(8,128)}, bf16[512,128]{1,0:T(8,128)(2,1)}, bf16[8,64,192]{2,1,0:T(8,128)(2,1)}) custom-call(f32[3]{0:T(128)} %skip_ref.1, bf16[192,2048]{1,0:T(8,128)(2,1)} %x_ref.3, bf16[192,2048]{1,0:T(8,128)(2,1)} %gate_ref.1, bf16[192,2048]{1,0:T(8,128)(2,1)} %res_ref.1, bf16[2048,128]{1,0:T(8,128)(2,1)} %in_ref.3, ...), custom_call_target="tpu_custom_call" | custom-call | tf_op jit(solution)/shard_map/local_ssd/pallas_call | solution.py:276
  57.7 0.0 all-to-all-done.2.in_ref
  57.7 0.0 copy-start.2
  57.7 8.5 %all-to-all-start.4 = ((bf16[8,64,192]{2,1,0:T(8,128)(2,1)}), bf16[8,64,192]{2,1,0:T(8,128)(2,1)S(1)}, u32[]{:S(2)}, u32[]{:S(2)}) async-start(bf16[8,64,192]{2,1,0:T(8,128)(2,1)} %get-tuple-element.18), calls=%async_computation.4 | async-start | bytes 524288 | tf_op jit(solution)/shard_map/all_to_all | solution.py:369
  66.1 0.0 copy-done.3
  66.1 0.6 reshape.10.gain_ref
  66.7 0.0 copy-done.2
  66.7 2.4 %gated.1 = bf16[8,64,256]{2,1,0:T(8,128)(2,1)} custom-call(bf16[8,24,128]{2,1,0:T(8,128)(2,1)} %copy-done.2, bf16[512,128]{1,0:T(8,128)(2,1)} %get-tuple-element.15.rows_ref, f32[512,192]{1,0:T(8,128)} %get-tuple-element.16.value_ref, f32[512,192]{1,0:T(8,128)} %get-tuple-element.17.factor_ref, bf16[1,192]{1,0:T(2,128)(2,1)} %reshape.10.gain_ref), custom_call_target="tpu_custom_call" | custom-call | tf_op jit(solution)/shard_map/gated/pallas_call | solution.py:276
  69.1 9.3 %all-to-all-done.4.res_ref = bf16[8,64,192]{2,1,0:T(8,128)(2,1)S(1)} async-done(((bf16[8,64,192]{2,1,0:T(8,128)(2,1)}), bf16[8,64,192]{2,1,0:T(8,128)(2,1)S(1)}, u32[]{:S(2)}, u32[]{:S(2)}) %all-to-all-start.4) | async-done | bytes 196640 | tf_op jit(solution)/shard_map/all_to_all | solution.py:369
  78.5 15.9 %all_to_all.27.in_ref = bf16[8,64,256]{2,1,0:T(8,128)(2,1)} all-to-all(bf16[8,64,256]{2,1,0:T(8,128)(2,1)} %gated.1), channel_id=1, replica_groups=mesh['y'=8,'x'=4,'core'=2,'head'=8] {'head'}, dimensions={0} | all-to-all | bytes 524288 | tf_op jit(solution)/shard_map/all_to_all | solution.py:377
  94.3 0.0 copy-done.1
  94.3 4.2 %project.1 = bf16[64,1536]{1,0:T(8,128)(2,1)} custom-call(bf16[8,64,256]{2,1,0:T(8,128)(2,1)} %all_to_all.27.in_ref, bf16[8,64,192]{2,1,0:T(8,128)(2,1)} %copy-done.1, bf16[2,1536,768]{2,1,0:T(8,128)(2,1)} %bitcast.2), custom_call_target="tpu_custom_call" | custom-call | tf_op jit(solution)/shard_map/project/pallas_call | solution.py:276
  (2 shorter events, 0.0 us)
Async XLA Ops:
  6.5 1.1 %copy-start = (bf16[192,1536]{1,0:T(8,128)(2,1)S(1)}, bf16[192,1536]{1,0:T(8,128)(2,1)}, u32[]{:S(2)}) copy-start(bf16[192,1536]{1,0:T(8,128)(2,1)} %param.21) | copy-start | bytes 1769476
  6.5 59.6 %copy-start.3 = (bf16[192]{0:T(256)(128)(2,1)S(1)}, bf16[192]{0:T(256)(128)(2,1)}, u32[]{:S(2)}) copy-start(bf16[192]{0:T(256)(128)(2,1)} %param.20) | copy-start | bytes 1156
  6.5 87.8 %all-gather.3.cloned.1.call-start = ((), (), s32[]{:S(2)}) async-start(), calls=%async_computation.5 | async-start | bytes 5013504 | tf_op jit(solution)/shard_map/all_gather | solution.py:314
  41.1 16.5 %all-to-all-start.2 = ((bf16[8,24,128]{2,1,0:T(8,128)(2,1)}), bf16[8,24,128]{2,1,0:T(8,128)(2,1)S(1)}, u32[]{:S(2)}, u32[]{:S(2)}) async-start(bf16[8,24,128]{2,1,0:T(8,128)(2,1)} %combine.1), calls=%async_computation.2 | async-start | bytes 98304 | tf_op jit(solution)/shard_map/all_to_all | solution.py:370
  57.7 9.0 %copy-start.2 = (bf16[8,24,128]{2,1,0:T(8,128)(2,1)}, bf16[8,24,128]{2,1,0:T(8,128)(2,1)S(1)}, u32[]{:S(2)}) copy-start(bf16[8,24,128]{2,1,0:T(8,128)(2,1)S(1)} %all-to-all-done.2.in_ref) | copy-start | bytes 147460
  57.7 20.8 %all-to-all-start.4 = ((bf16[8,64,192]{2,1,0:T(8,128)(2,1)}), bf16[8,64,192]{2,1,0:T(8,128)(2,1)S(1)}, u32[]{:S(2)}, u32[]{:S(2)}) async-start(bf16[8,64,192]{2,1,0:T(8,128)(2,1)} %get-tuple-element.18), calls=%async_computation.4 | async-start | bytes 524288 | tf_op jit(solution)/shard_map/all_to_all | solution.py:369
  78.5 15.9 %copy-start.1 = (bf16[8,64,192]{2,1,0:T(8,128)(2,1)}, bf16[8,64,192]{2,1,0:T(8,128)(2,1)S(1)}, u32[]{:S(2)}) copy-start(bf16[8,64,192]{2,1,0:T(8,128)(2,1)S(1)} %all-to-all-done.4.res_ref) | copy-start | bytes 589828
Sparse Core Ops, SparseCore 0:
  9.5 51.2 all-gather.2

commit v2 on v1

--- a/solution.py
+++ b/solution.py
@@ -128,103 +128,121 @@
         out_ref[i] = (before_ref[i] + factor_ref[i] * state).astype(BF16)
 
 
-def local_kernel(
+def ranks(flag_ref):
+    chunks = flag_ref.shape[0]
+    flags = flag_ref[...].astype(F32)
+    within = dot(flags.astype(BF16), below((Q, Q)))
+    sums = jnp.broadcast_to(within[:, Q - 1 : Q], (chunks, Q)).astype(BF16)
+    earlier = dot(below((chunks, chunks), strict=True).T, sums)
+    return jnp.where(flags > 0.0, within + earlier, 0.0) - 1.0
+
+
+def fill_pick(pick, flag_ref):
+    rank = ranks(flag_ref)
+    slot = lax.broadcasted_iota(jnp.int32, (Q, Q), 0).astype(F32)
+    for g in range(pick.shape[0] // Q):
+        for c in range(flag_ref.shape[0]):
+            hit = (rank[c : c + 1] - float(g * Q)) == slot
+            pick[g * Q : (g + 1) * Q, c * Q : (c + 1) * Q] = jnp.where(hit, 1.0, 0.0).astype(BF16)
+
+
+def pick_kernel(
+    heads,
+    gate_ref,
+    res_ref,
+    out_map_ref,
+    decay_ref,
+    flag_ref,
+    silu_ref,
+    factor_ref,
+    rows_ref,
+    picked_ref,
+    cums,
+    pick,
+):
+    width = gate_ref.shape[0] // heads
+    chunks = flag_ref.shape[0]
+    run_row = dot3(chunk_rows(decay_ref, heads), below((Q, Q)))
+    before = jnp.zeros((heads, 1), F32)
+    for c in range(chunks):
+        run = run_row[c * heads : (c + 1) * heads]
+        for i, piece in enumerate(pieces(run + before)):
+            cums[i * 8 : i * 8 + heads, c * Q : (c + 1) * Q] = piece.astype(F32)
+        before = before + run[:, Q - 1 : Q]
+    fill_pick(pick, flag_ref)
+    log_pieces = cums[...].astype(BF16)
+    per = picked_ref.shape[1]
+    step = min(per, Q)
+    for g in range(pick.shape[0] // Q):
+        these = slice(g * Q, (g + 1) * Q)
+        chosen = pick[these]
+        gate = dot(chosen, gate_ref[...], NT)
+        silu_ref[these] = gate / (1.0 + jnp.exp(-gate))
+        logs_at = dot(chosen, log_pieces, NT)
+        for h in range(heads):
+            run = logs_at[:, h : h + 1] + logs_at[:, 8 + h : 9 + h] + logs_at[:, 16 + h : 17 + h]
+            factor_ref[these, h * width : (h + 1) * width] = jnp.broadcast_to(
+                jnp.exp(run), (Q, width)
+            )
+        rows_ref[these] = dot(chosen, out_map_ref[...]).astype(BF16)
+        taken = dot(chosen, res_ref[...], NT).astype(BF16)
+        for j in range(0, Q, step):
+            to, at = divmod(g * Q + j, per)
+            picked_ref[to, at : at + step] = taken[j : j + step]
+
+
+def ssd_kernel(
     heads,
     skip_ref,
     x_ref,
-    gate_ref,
-    res_ref,
     in_ref,
     out_map_ref,
     step_ref,
     decay_ref,
     flag_ref,
     value_ref,
-    factor_ref,
-    rows_ref,
-    picked_ref,
     y_all,
-    cums,
+    scaled,
+    state,
     pick,
 ):
     width = x_ref.shape[0] // heads
-    length = x_ref.shape[1]
-    chunks = length // Q
-    upto = below((Q, Q))
+    chunks = flag_ref.shape[0]
     row = lax.broadcasted_iota(jnp.int32, (Q, Q), 0)
     col = lax.broadcasted_iota(jnp.int32, (Q, Q), 1)
     mask = row <= col
-    eye = jnp.where(row == col, 1.0, 0.0).astype(BF16)
-    down = jnp.where(col <= row, 1.0, 0.0).astype(BF16)
     logs = chunk_rows(decay_ref, heads)
-    steps = chunk_rows(step_ref, heads)
-    run_row = dot3(logs, upto)
-    run_col = dot3r(down, logs)
-    step_col = dot3r(eye, steps)
-    state = [jnp.zeros((width, Q), F32) for _ in range(heads)]
-    before = [jnp.zeros((1, 1), F32) for _ in range(heads)]
+    run_row = dot3(logs, below((Q, Q)))
+    run_col = dot3r(jnp.where(col <= row, 1.0, 0.0).astype(BF16), logs)
+    state[...] = jnp.zeros_like(state)
     for c in range(chunks):
         lanes = slice(c * Q, (c + 1) * Q)
         b = in_ref[lanes, :]
         o = out_map_ref[lanes, :]
         scores = dot(b, o, NT)
+        outer = dot(state[...].astype(BF16), o, NT)
         for h in range(heads):
             k = c * heads + h
             part = slice(h * width, (h + 1) * width)
             run = run_row[k : k + 1]
             last = run[:, Q - 1 : Q]
-            spread_log = run - run_col[:, k : k + 1]
-            decay = jnp.where(mask, jnp.exp(spread_log), 0.0)
-            weights = (scores * decay * step_col[:, k : k + 1]).astype(BF16)
-            x = x_ref[part, lanes]
-            xf = x.astype(F32)
-            y = dot(x, weights) + skip_ref[h] * xf
-            y = y + dot(state[h].astype(BF16), o, NT) * jnp.exp(run)
-            y_all[part, lanes] = y.astype(BF16)
-            scaled = (xf * (steps[k : k + 1] * jnp.exp(last - run))).astype(BF16)
-            state[h] = jnp.exp(last) * state[h] + dot(scaled, b)
-            for i, piece in enumerate(pieces(run + before[h])):
-                cums[i * 8 + h : i * 8 + h + 1, lanes] = piece.astype(F32)
-            before[h] = before[h] + last
-
-    flags = flag_ref[...].astype(F32)
-    within = dot(flags.astype(BF16), upto)
-    rows = lax.broadcasted_iota(jnp.int32, (chunks, chunks), 0)
-    cols = lax.broadcasted_iota(jnp.int32, (chunks, chunks), 1)
-    sums = jnp.broadcast_to(within[:, Q - 1 : Q], (chunks, Q)).astype(BF16)
-    earlier = dot(jnp.where(cols < rows, 1.0, 0.0).astype(BF16), sums)
-    rank = jnp.where(flags > 0.0, within + earlier, 0.0) - 1.0
-    slots = value_ref.shape[0]
-    tile = 128
-    slot = lax.broadcasted_iota(jnp.int32, (tile, Q), 0).astype(F32)
-    for g in range(slots // tile):
-        for c in range(chunks):
-            hit = (rank[c : c + 1] - float(g * tile)) == slot
-            pick[g * tile : (g + 1) * tile, c * Q : (c + 1) * Q] = jnp.where(hit, 1.0, 0.0).astype(
-                BF16
-            )
-    log_pieces = cums[...].astype(BF16)
-    for g in range(slots // tile):
-        these = slice(g * tile, (g + 1) * tile)
-        chosen = pick[these]
-        gate = dot(chosen, gate_ref[...], NT)
-        silu = gate / (1.0 + jnp.exp(-gate))
-        value_ref[these] = dot(chosen, y_all[...], NT) * silu
-        logs_at = dot(chosen, log_pieces, NT)
-        for h in range(heads):
-            run = logs_at[:, h : h + 1] + logs_at[:, 8 + h : 9 + h] + logs_at[:, 16 + h : 17 + h]
-            part = slice(h * width, (h + 1) * width)
-            factor_ref[these, part] = jnp.exp(run) * silu[:, part]
-        rows_ref[these] = dot(chosen, out_map_ref[...]).astype(BF16)
-        per = picked_ref.shape[1]
-        taken = dot(chosen, res_ref[...], NT).astype(BF16)
-        step = min(per, tile)
-        for j in range(0, tile, step):
-            to, at = divmod(g * tile + j, per)
-            picked_ref[to, at : at + step] = taken[j : j + step]
-
-
-def gate_kernel(heads, in_ref, rows_ref, value_ref, factor_ref, gain_ref, out_ref):
+            decay = jnp.where(mask, jnp.exp(run - run_col[:, k : k + 1]), 0.0)
+            weights = (scores * decay).astype(BF16)
+            xf = x_ref[part, lanes].astype(F32)
+            stepped = xf * step_ref[h : h + 1, lanes]
+            y = dot(stepped.astype(BF16), weights) + skip_ref[h] * xf
+            y_all[part, lanes] = (y + outer[part] * jnp.exp(run)).astype(BF16)
+            scaled[part] = (stepped * jnp.exp(last - run)).astype(BF16)
+            state[part] = state[part] * jnp.exp(last)
+        if c < chunks - 1:
+            state[...] += dot(scaled[...], b)
+    fill_pick(pick, flag_ref)
+    for g in range(pick.shape[0] // Q):
+        these = slice(g * Q, (g + 1) * Q)
+        value_ref[these] = dot(pick[these], y_all[...], NT)
+
+
+def gate_kernel(heads, in_ref, rows_ref, value_ref, factor_ref, silu_ref, gain_ref, out_ref):
     parts = in_ref.shape[0]
     rows = in_ref.shape[1] // heads
     per = out_ref.shape[1]
@@ -233,7 +251,7 @@
     states = [held[:, h * rows : (h + 1) * rows].reshape(parts * rows, Q) for h in range(heads)]
     incoming = jnp.concatenate(states, axis=0).astype(BF16)
     outer = dot(rows_ref[...], incoming, NT)
-    gated = value_ref[...] + factor_ref[...] * outer
+    gated = (value_ref[...] + factor_ref[...] * outer) * silu_ref[...]
     squares = jnp.sum(gated * gated, axis=1, keepdims=True)
     scaled = (gated * gain_ref[...].astype(F32)).astype(BF16)
     slots = gated.shape[0]
@@ -269,7 +287,7 @@
         out_ref[:, part] = (done * scale + res[:, part].astype(F32)).astype(BF16)
 
 
-def call(kernel, outs, args, scratch=(), smem=0, name=None):
+def call(kernel, outs, args, scratch=(), smem=0, name=None, mib=4):
     vmem = pl.BlockSpec(memory_space=pltpu.VMEM)
     specs = [pl.BlockSpec(memory_space=pltpu.SMEM)] * smem + [vmem] * (len(args) - smem)
     many = isinstance(outs, (tuple, list))
@@ -279,6 +297,7 @@
         in_specs=specs,
         out_specs=[vmem] * len(outs) if many else vmem,
         scratch_shapes=list(scratch),
+        compiler_params=pltpu.CompilerParams(vmem_limit_bytes=mib << 20),
         name=name,
     )(*args)
 
@@ -309,10 +328,8 @@
     used = local_width // parts
     height = used + 8
 
-    half = full_width // lax.axis_size("core")
-    own = lax.dynamic_slice_in_dim(out_weight, lax.axis_index("core") * half, half, 1)
-    weight = lax.all_gather(own[None], ("core", "head"), axis=0, tiled=True)
-    weight = weight.reshape(lax.axis_size("core"), shares * local_width, half)
+    held = lax.optimization_barrier
+    flags = boundary.reshape(length // Q, Q)
 
     state = call(
         functools.partial(final_state_kernel, heads, parts),
@@ -320,8 +337,28 @@
         (head_input, input_map, step_size, log_decay),
         [pltpu.VMEM((local_width, length), BF16)],
         name="final_state",
-    )
+        mib=8,
+    )
+    state, flags, out_weight = held((state, flags, out_weight))
+    half = full_width // lax.axis_size("core")
+    own = lax.dynamic_slice_in_dim(out_weight, lax.axis_index("core") * half, half, 1)
+    weight = lax.all_gather(own[None], ("core", "head"), axis=0, tiled=True)
+    weight = weight.reshape(lax.axis_size("core"), shares * local_width, half)
     moved = lax.all_to_all(state, group, 0, 0, tiled=True)
+    silu, since, rows, picked = call(
+        functools.partial(pick_kernel, heads),
+        (
+            S((slots, local_width), F32),
+            S((slots, local_width), F32),
+            S((slots, Q), BF16),
+            S((shares, per, local_width), BF16),
+        ),
+        (gate_input, residual, output_map, log_decay, flags),
+        [pltpu.VMEM((24, length), F32), pltpu.VMEM((slots, length), BF16)],
+        name="pick",
+        mib=12,
+    )
+    moved, picked = held((moved, picked))
     before, factor, total = call(
         functools.partial(group_scan_kernel, heads),
         (
@@ -332,47 +369,37 @@
         (moved,),
         name="group_scan",
     )
+    total, flags, picked = held((total, flags, picked))
     totals = lax.all_to_all(total, "y", 0, 0, tiled=True)
-    value, decay, rows, picked = call(
-        functools.partial(local_kernel, heads),
-        (
-            S((slots, local_width), F32),
-            S((slots, local_width), F32),
-            S((slots, Q), BF16),
-            S((shares, per, local_width), BF16),
-        ),
-        (
-            skip_gain,
-            head_input,
-            gate_input,
-            residual,
-            input_map,
-            output_map,
-            step_size,
-            log_decay,
-            boundary.reshape(length // Q, Q),
-        ),
+    kept = lax.all_to_all(picked, "head", 0, 0, tiled=True)
+    value = call(
+        functools.partial(ssd_kernel, heads),
+        S((slots, local_width), F32),
+        (skip_gain, head_input, input_map, output_map, step_size, log_decay, flags),
         [
             pltpu.VMEM((local_width, length), BF16),
-            pltpu.VMEM((24, length), F32),
+            pltpu.VMEM((local_width, Q), BF16),
+            pltpu.VMEM((local_width, Q), F32),
             pltpu.VMEM((slots, length), BF16),
         ],
         smem=1,
-        name="local_ssd",
-    )
+        name="ssd",
+        mib=12,
+    )
+    totals, value = held((totals, value))
     incoming = call(
         functools.partial(combine_kernel, heads),
         S((parts, used, Q), BF16),
         (totals, before, factor),
         name="combine",
     )
-    kept = lax.all_to_all(picked, "head", 0, 0, tiled=True)
     incoming = lax.all_to_all(incoming, group, 0, 0, tiled=True)
     gated = call(
         functools.partial(gate_kernel, heads),
         S((shares, per, -(-(local_width + 3) // Q) * Q), BF16),
-        (incoming, rows, value, decay, norm_gain.reshape(1, local_width)),
+        (incoming, rows, value, since, silu, norm_gain.reshape(1, local_width)),
         name="gated",
+        mib=6,
     )
     gathered = lax.all_to_all(gated, "head", 0, 0, tiled=True)
     return call(
@@ -381,6 +408,7 @@
         (gathered, kept, weight),
         [pltpu.VMEM((per, full_width), BF16), pltpu.VMEM((per, full_width), BF16)],
         name="project",
+        mib=10,
     )
 
 

time: 106 us -> 104 us (0.981); the launches traced: 105 us -> 101 us
  blocking collectives: 42.7 us -> 22.6 us
  local copies, waits for them, and re-layouts: 2.39 us -> 18.8 us
  Pallas kernels: 23.9 us -> 13.8 us
  starting transfers between devices: 13.6 us -> 23 us
    unnamed x8 -> x56, local copies, waits for them, and re-layouts: 1.07 us -> 18 us
    all_to_all x2 -> x1, blocking collectives: 26.9 us -> 10.7 us  [on_device(): incoming = lax.all_to_all(incoming, group, 0, 0, tiled=True)]
    pallas_call x6 -> x7, Pallas kernels: 23.9 us -> 13.8 us  [call(): pl.pallas_call(kernel, out_shape=outs, in_specs=specs, out_specs=[vmem] *...]
    all_to_all x1 -> x2, starting transfers between devices: 5.1 us -> 14.1 us  [the longest x1 10.1 us: on_device(): moved = lax.all_to_all(state, group, 0, 0, tiled=True)]
    all_to_all x1, blocking collectives: 15.9 us -> 12 us  [on_device(): gathered = lax.all_to_all(gated, 'head', 0, 0, tiled=True)]
    all_to_all x1 -> x2, waiting for transfers between devices: 0.01 us -> 1.83 us  [the longest x1 1.82 us: on_device(): totals = lax.all_to_all(total, 'y', 0, 0, tiled=True)]
    all_to_all x1, waiting for transfers between devices: 9.33 us -> 7.93 us  [on_device(): kept = lax.all_to_all(picked, 'head', 0, 0, tiled=True)]
  transfers between devices with their start and end apart: 3 -> 4, of which waited for: 1 -> 2; matrix products, arithmetic and copies ran while one was open for 1% -> 0% of each run, Pallas kernels for 19% -> 11%
where the time goes in v2:
time: 104 us; the launch traced here: 101 us
  starting transfers between devices  23 us (22%)
  blocking collectives  22.6 us (22%)
  local copies, waits for them, and re-layouts  18.8 us (18%)
  Pallas kernels  13.8 us (13%)
  between operations  13.6 us (13%)
  waiting for transfers between devices  9.77 us (9%)
    unnamed x56, local copies, waits for them, and re-layouts  18 us
    pallas_call x7, Pallas kernels, call(): pl.pallas_call(kernel, out_shape=outs, in_specs=specs, out_specs=[vmem] *...  13.8 us
    all_to_all x1, blocking collectives, on_device(): gathered = lax.all_to_all(gated, 'head', 0, 0, tiled=True)  12 us
    all_to_all x1, blocking collectives, on_device(): incoming = lax.all_to_all(incoming, group, 0, 0, tiled=True)  10.7 us
    all_to_all x1, starting transfers between devices, on_device(): moved = lax.all_to_all(state, group, 0, 0, tiled=True)  10.1 us
    all_to_all x1, starting transfers between devices, on_device(): kept = lax.all_to_all(picked, 'head', 0, 0, tiled=True)  8.88 us
    all_to_all x1, waiting for transfers between devices, on_device(): kept = lax.all_to_all(picked, 'head', 0, 0, tiled=True)  7.93 us
    all_to_all x1, starting transfers between devices, on_device(): totals = lax.all_to_all(total, 'y', 0, 0, tiled=True)  3.97 us
  transfers between devices with their start and end apart: 4, of which 2 were waited for; matrix products, arithmetic and copies ran while one was open for 0% of the time, Pallas kernels for 11%

profile of v2, /device:TPU:1, one launch (start us, length us, event | category | flops | bytes accessed | tf_op | source)
XLA Modules:
  0.0 101.5 jit_solution(2902225021914102947)
XLA Ops:
  6.6 1.2 %copy-done.2 = bf16[192,2048]{1,0:T(8,128)(2,1)S(1)} copy-done((bf16[192,2048]{1,0:T(8,128)(2,1)S(1)}, bf16[192,2048]{1,0:T(8,128)(2,1)}, u32[]{:S(2)}) %copy-start.2) | copy-done | bytes 786456
  7.7 1.0 %copy-done.4 = bf16[2048,128]{1,0:T(8,128)(2,1)S(1)} copy-done((bf16[2048,128]{1,0:T(8,128)(2,1)S(1)}, bf16[2048,128]{1,0:T(8,128)(2,1)}, u32[]{:S(2)}) %copy-start.4) | copy-done | bytes 524312
  8.8 0.8 copy-done.12
  10.3 1.2 %final_state.1 = bf16[8,32,128]{2,1,0:T(8,128)(2,1)} custom-call(bf16[192,2048]{1,0:T(8,128)(2,1)S(1)} %copy-done.2, bf16[2048,128]{1,0:T(8,128)(2,1)S(1)} %copy-done.4, f32[3,2048]{1,0:T(4,128)S(1)} %copy-done.16, f32[3,2048]{1,0:T(4,128)S(1)} %copy-done.12), custom_call_target="tpu_custom_call" | custom-call | tf_op jit(solution)/shard_map/final_state/pallas_call | solution.py:294
  12.3 10.1 %all-to-all-start = ((bf16[8,32,128]{2,1,0:T(8,128)(2,1)}), bf16[8,32,128]{2,1,0:T(8,128)(2,1)S(1)}, u32[]{:S(2)}, u32[]{:S(2)}) async-start(bf16[8,32,128]{2,1,0:T(8,128)(2,1)} %final_state.1), calls=%async_computation | async-start | bytes 131072 | tf_op jit(solution)/shard_map/all_to_all | solution.py:347
  22.4 1.0 %copy-done.6 = bf16[2048,128]{1,0:T(8,128)(2,1)S(1)} copy-done((bf16[2048,128]{1,0:T(8,128)(2,1)S(1)}, bf16[2048,128]{1,0:T(8,128)(2,1)}, u32[]{:S(2)}) %copy-start.6) | copy-done | bytes 524312
  23.5 1.1 %copy-done.8 = bf16[192,2048]{1,0:T(8,128)(2,1)S(1)} copy-done((bf16[192,2048]{1,0:T(8,128)(2,1)S(1)}, bf16[192,2048]{1,0:T(8,128)(2,1)}, u32[]{:S(2)}) %copy-start.8) | copy-done | bytes 786456
  24.6 1.1 %copy-done.9 = bf16[192,2048]{1,0:T(8,128)(2,1)S(1)} copy-done((bf16[192,2048]{1,0:T(8,128)(2,1)S(1)}, bf16[192,2048]{1,0:T(8,128)(2,1)}, u32[]{:S(2)}) %copy-start.9) | copy-done | bytes 786456
  27.2 3.5 %pick.1 = (f32[512,192]{1,0:T(8,128)S(1)}, f32[512,192]{1,0:T(8,128)S(1)}, bf16[512,128]{1,0:T(8,128)(2,1)S(1)}, bf16[8,64,192]{2,1,0:T(8,128)(2,1)S(1)}) custom-call(bf16[192,2048]{1,0:T(8,128)(2,1)S(1)} %copy-done.8, bf16[192,2048]{1,0:T(8,128)(2,1)S(1)} %copy-done.9, bf16[2048,128]{1,0:T(8,128)(2,1)S(1)} %copy-done.6, f32[3,2048]{1,0:T(4,128)S(1)} %copy-done.13, ...), custom_call_target="tpu_custom_call" | custom-call | tf_op jit(solution)/shard_map/pick/pallas_call | solution.py:294
  30.7 0.8 copy-done.10
  34.9 4.0 %all-to-all-start.1 = ((bf16[8,32,128]{2,1,0:T(8,128)(2,1)}), bf16[8,32,128]{2,1,0:T(8,128)(2,1)}, u32[]{:S(2)}, u32[]{:S(2)}) async-start(bf16[8,32,128]{2,1,0:T(8,128)(2,1)} %get-tuple-element.28), calls=%async_computation.1 | async-start | bytes 131072 | tf_op jit(solution)/shard_map/all_to_all | solution.py:373
  38.9 5.3 %ssd.1.value_ref = f32[512,192]{1,0:T(8,128)S(1)} custom-call(f32[3]{0:T(128)S(1)} %copy-done.26, bf16[192,2048]{1,0:T(8,128)(2,1)S(1)} %copy-done.3, bf16[2048,128]{1,0:T(8,128)(2,1)S(1)} %copy-done.5, bf16[2048,128]{1,0:T(8,128)(2,1)S(1)} %copy-done.7, f32[3,2048]{1,0:T(4,128)S(1)} %copy-done.17, f32[3,2048]{1,0:T(4,128)S(1)} %copy-done.14, ...), custom_call_target="tpu_custom_call" | custom-call | tf_op jit(solution)/shard_map/ssd/pallas_call | solution.py:294
  44.2 1.8 %all-to-all-done.1.in_ref = bf16[8,32,128]{2,1,0:T(8,128)(2,1)} async-done(((bf16[8,32,128]{2,1,0:T(8,128)(2,1)}), bf16[8,32,128]{2,1,0:T(8,128)(2,1)}, u32[]{:S(2)}, u32[]{:S(2)}) %all-to-all-start.1) | async-done | bytes 65568 | tf_op jit(solution)/shard_map/all_to_all | solution.py:373
  46.0 0.9 copy-done.21
  46.9 0.9 copy-done.23
  47.8 0.9 combine.1
  48.8 10.7 %all_to_all.25.in_ref = bf16[8,24,128]{2,1,0:T(8,128)(2,1)S(1)} all-to-all(bf16[8,24,128]{2,1,0:T(8,128)(2,1)S(1)} %combine.1), channel_id=1, replica_groups=mesh['y'=8,'x'=4,'core'=2,'head'=8] {'x','core'}, dimensions={0} | all-to-all | bytes 98304 | tf_op jit(solution)/shard_map/all_to_all | solution.py:396
  59.4 8.9 %all-to-all-start.4 = ((bf16[8,64,192]{2,1,0:T(8,128)(2,1)}), bf16[8,64,192]{2,1,0:T(8,128)(2,1)S(1)}, u32[]{:S(2)}, u32[]{:S(2)}) async-start(bf16[8,64,192]{2,1,0:T(8,128)(2,1)} %copy-done.15), calls=%async_computation.4 | async-start | bytes 524288 | tf_op jit(solution)/shard_map/all_to_all | solution.py:374
  68.3 1.0 %copy-done.11 = f32[512,192]{1,0:T(8,128)S(1)} copy-done((f32[512,192]{1,0:T(8,128)S(1)}, f32[512,192]{1,0:T(8,128)}, u32[]{:S(2)}) %copy-start.11) | copy-done | bytes 393240
  69.4 0.9 copy-done.19
  70.7 7.9 %all-to-all-done.4.res_ref = bf16[8,64,192]{2,1,0:T(8,128)(2,1)S(1)} async-done(((bf16[8,64,192]{2,1,0:T(8,128)(2,1)}), bf16[8,64,192]{2,1,0:T(8,128)(2,1)S(1)}, u32[]{:S(2)}, u32[]{:S(2)}) %all-to-all-start.4) | async-done | bytes 196640 | tf_op jit(solution)/shard_map/all_to_all | solution.py:374
  78.7 12.0 %all_to_all.26.in_ref = bf16[8,64,256]{2,1,0:T(8,128)(2,1)S(1)} all-to-all(bf16[8,64,256]{2,1,0:T(8,128)(2,1)S(1)} %gated.1), channel_id=1, replica_groups=mesh['y'=8,'x'=4,'core'=2,'head'=8] {'head'}, dimensions={0} | all-to-all | bytes 524288 | tf_op jit(solution)/shard_map/all_to_all | solution.py:404
  90.6 2.3 %copy-done.1 = bf16[3072,768]{1,0:T(8,128)(2,1)S(1)} copy-done((bf16[3072,768]{1,0:T(8,128)(2,1)S(1)}, bf16[3072,768]{1,0:T(8,128)(2,1)}, u32[]{:S(2)}) %copy-start.1) | copy-done | bytes 4718616
  93.0 1.7 %project.1 = bf16[64,1536]{1,0:T(8,128)(2,1)} custom-call(bf16[8,64,256]{2,1,0:T(8,128)(2,1)S(1)} %all_to_all.26.in_ref, bf16[8,64,192]{2,1,0:T(8,128)(2,1)S(1)} %all-to-all-done.4.res_ref, bf16[2,1536,768]{2,1,0:T(8,128)(2,1)S(1)} %bitcast.2), custom_call_target="tpu_custom_call" | custom-call | tf_op jit(solution)/shard_map/project/pallas_call | solution.py:294
  (52 shorter events, 6.8 us)
Async XLA Ops:
  6.5 5.0 %copy-start = (bf16[192,1536]{1,0:T(8,128)(2,1)S(1)}, bf16[192,1536]{1,0:T(8,128)(2,1)}, u32[]{:S(2)}) copy-start(bf16[192,1536]{1,0:T(8,128)(2,1)} %param.21) | copy-start | bytes 1769476
  6.5 32.3 %copy-start.26 = (f32[3]{0:T(128)S(1)}, f32[3]{0:T(128)}, u32[]{:S(2)}) copy-start(f32[3]{0:T(128)} %skip_ref.1) | copy-start | bytes 40
  6.5 61.8 %copy-start.27 = (bf16[192]{0:T(256)(128)(2,1)S(1)}, bf16[192]{0:T(256)(128)(2,1)}, u32[]{:S(2)}) copy-start(bf16[192]{0:T(256)(128)(2,1)} %param.20) | copy-start | bytes 1156
  6.5 84.1 %all-gather.3.cloned.1.call-start = ((), (), s32[]{:S(2)}) async-start(), calls=%async_computation.5 | async-start | bytes 5013504 | tf_op jit(solution)/shard_map/all_gather | solution.py:345
  6.6 1.2 %copy-start.2 = (bf16[192,2048]{1,0:T(8,128)(2,1)S(1)}, bf16[192,2048]{1,0:T(8,128)(2,1)}, u32[]{:S(2)}) copy-start(bf16[192,2048]{1,0:T(8,128)(2,1)} %x_ref.3) | copy-start | bytes 2359300
  7.7 1.0 %copy-start.4 = (bf16[2048,128]{1,0:T(8,128)(2,1)S(1)}, bf16[2048,128]{1,0:T(8,128)(2,1)}, u32[]{:S(2)}) copy-start(bf16[2048,128]{1,0:T(8,128)(2,1)} %in_ref.3) | copy-start | bytes 1572868
  10.3 28.5 %copy-start.3 = (bf16[192,2048]{1,0:T(8,128)(2,1)S(1)}, bf16[192,2048]{1,0:T(8,128)(2,1)}, u32[]{:S(2)}) copy-start(bf16[192,2048]{1,0:T(8,128)(2,1)} %x_ref.3) | copy-start | bytes 2359300
  10.3 28.6 %copy-start.5 = (bf16[2048,128]{1,0:T(8,128)(2,1)S(1)}, bf16[2048,128]{1,0:T(8,128)(2,1)}, u32[]{:S(2)}) copy-start(bf16[2048,128]{1,0:T(8,128)(2,1)} %in_ref.3) | copy-start | bytes 1572868
  10.3 28.6 %copy-start.7 = (bf16[2048,128]{1,0:T(8,128)(2,1)S(1)}, bf16[2048,128]{1,0:T(8,128)(2,1)}, u32[]{:S(2)}) copy-start(bf16[2048,128]{1,0:T(8,128)(2,1)} %out_map_ref.3) | copy-start | bytes 1572868
  10.3 28.6 %copy-start.14 = (f32[3,2048]{1,0:T(4,128)S(1)}, f32[3,2048]{1,0:T(4,128)}, u32[]{:S(2)}) copy-start(f32[3,2048]{1,0:T(4,128)} %decay_ref.5) | copy-start | bytes 73732
  10.3 28.6 %copy-start.17 = (f32[3,2048]{1,0:T(4,128)S(1)}, f32[3,2048]{1,0:T(4,128)}, u32[]{:S(2)}) copy-start(f32[3,2048]{1,0:T(4,128)} %step_ref.3) | copy-start | bytes 73732
  10.3 28.6 %copy-start.25 = (s32[2048]{0:T(1024)S(1)}, s32[2048]{0:T(1024)}, u32[]{:S(2)}) copy-start(s32[2048]{0:T(1024)} %param.19) | copy-start | bytes 24580
  12.3 20.5 %all-to-all-start = ((bf16[8,32,128]{2,1,0:T(8,128)(2,1)}), bf16[8,32,128]{2,1,0:T(8,128)(2,1)S(1)}, u32[]{:S(2)}, u32[]{:S(2)}) async-start(bf16[8,32,128]{2,1,0:T(8,128)(2,1)} %final_state.1), calls=%async_computation | async-start | bytes 131072 | tf_op jit(solution)/shard_map/all_to_all | solution.py:347
  22.4 1.0 %copy-start.6 = (bf16[2048,128]{1,0:T(8,128)(2,1)S(1)}, bf16[2048,128]{1,0:T(8,128)(2,1)}, u32[]{:S(2)}) copy-start(bf16[2048,128]{1,0:T(8,128)(2,1)} %out_map_ref.3) | copy-start | bytes 1572868
  23.5 1.1 %copy-start.8 = (bf16[192,2048]{1,0:T(8,128)(2,1)S(1)}, bf16[192,2048]{1,0:T(8,128)(2,1)}, u32[]{:S(2)}) copy-start(bf16[192,2048]{1,0:T(8,128)(2,1)} %gate_ref.1) | copy-start | bytes 2359300
  24.6 1.1 %copy-start.9 = (bf16[192,2048]{1,0:T(8,128)(2,1)S(1)}, bf16[192,2048]{1,0:T(8,128)(2,1)}, u32[]{:S(2)}) copy-start(bf16[192,2048]{1,0:T(8,128)(2,1)} %res_ref.1) | copy-start | bytes 2359300
  30.7 0.8 copy-start.10
  34.9 11.2 %all-to-all-start.1 = ((bf16[8,32,128]{2,1,0:T(8,128)(2,1)}), bf16[8,32,128]{2,1,0:T(8,128)(2,1)}, u32[]{:S(2)}, u32[]{:S(2)}) async-start(bf16[8,32,128]{2,1,0:T(8,128)(2,1)} %get-tuple-element.28), calls=%async_computation.1 | async-start | bytes 131072 | tf_op jit(solution)/shard_map/all_to_all | solution.py:373
  46.0 0.9 copy-start.21
  46.9 0.9 copy-start.23
  59.4 19.2 %all-to-all-start.4 = ((bf16[8,64,192]{2,1,0:T(8,128)(2,1)}), bf16[8,64,192]{2,1,0:T(8,128)(2,1)S(1)}, u32[]{:S(2)}, u32[]{:S(2)}) async-start(bf16[8,64,192]{2,1,0:T(8,128)(2,1)} %copy-done.15), calls=%async_computation.4 | async-start | bytes 524288 | tf_op jit(solution)/shard_map/all_to_all | solution.py:374
  68.3 1.0 %copy-start.11 = (f32[512,192]{1,0:T(8,128)S(1)}, f32[512,192]{1,0:T(8,128)}, u32[]{:S(2)}) copy-start(f32[512,192]{1,0:T(8,128)} %copy-done.10) | copy-start | bytes 1179652
  69.4 0.9 copy-start.19
  90.6 2.3 %copy-start.1 = (bf16[3072,768]{1,0:T(8,128)(2,1)S(1)}, bf16[3072,768]{1,0:T(8,128)(2,1)}, u32[]{:S(2)}) copy-start(bf16[3072,768]{1,0:T(8,128)(2,1)} %all-gather.3.cloned.1.call-done) | copy-start | bytes 14155780
  (8 other events, 5.6 us)
Sparse Core Ops, SparseCore 0:
  12.4 51.1 all-gather.2

commit v3 on v2

--- a/solution.py
+++ b/solution.py
@@ -58,18 +58,20 @@
     return jnp.concatenate([tile, jnp.zeros((rows - heads, Q), F32)], axis=0)
 
 
-def final_state_kernel(heads, parts, x_ref, in_ref, step_ref, decay_ref, out_ref, scaled):
-    width = x_ref.shape[0] // heads
-    length = x_ref.shape[1]
+def final_state_kernel(heads, parts, x, in_map, step, decay, out_ref, scaled):
+    width = x.shape[0] // heads
+    length = x.shape[1]
     chunks = length // Q
     rows = width // parts
-    logs = chunk_rows(decay_ref, heads)
+    logs = chunk_rows(decay(), heads)
     after = lax.broadcasted_iota(jnp.int32, (Q, Q), 0) > lax.broadcasted_iota(
         jnp.int32, (Q, Q), 1
     )
     suffix = dot3(logs, jnp.where(after, 1.0, 0.0).astype(BF16))
     sums = jnp.sum(logs, axis=1, keepdims=True)
     later = jnp.zeros((heads, 1), F32)
+    step_ref = step()
+    x_ref = x()
     for c in reversed(range(chunks)):
         here = slice(c * heads, (c + 1) * heads)
         lanes = slice(c * Q, (c + 1) * Q)
@@ -78,7 +80,7 @@
             part = slice(h * width, (h + 1) * width)
             scaled[part, lanes] = (x_ref[part, lanes].astype(F32) * factor[h : h + 1]).astype(BF16)
         later = later + sums[here]
-    state = dot(scaled[...], in_ref[...])
+    state = dot(scaled[...], in_map()[...])
     tail = log_tile(later, out_ref.shape[1] - heads * rows)
     for j in range(parts):
         own = [state[h * width + j * rows : h * width + (j + 1) * rows] for h in range(heads)]
@@ -148,73 +150,80 @@
 
 def pick_kernel(
     heads,
-    gate_ref,
-    res_ref,
-    out_map_ref,
-    decay_ref,
-    flag_ref,
-    silu_ref,
-    factor_ref,
-    rows_ref,
-    picked_ref,
+    gate,
+    res,
+    out_map,
+    decay,
+    flags,
+    silu_out,
+    factor_out,
+    rows_out,
+    picked_out,
     cums,
     pick,
 ):
-    width = gate_ref.shape[0] // heads
+    width = gate.shape[0] // heads
+    flag_ref = flags()
     chunks = flag_ref.shape[0]
-    run_row = dot3(chunk_rows(decay_ref, heads), below((Q, Q)))
+    fill_pick(pick, flag_ref)
+    run_row = dot3(chunk_rows(decay(), heads), below((Q, Q)))
     before = jnp.zeros((heads, 1), F32)
     for c in range(chunks):
         run = run_row[c * heads : (c + 1) * heads]
         for i, piece in enumerate(pieces(run + before)):
             cums[i * 8 : i * 8 + heads, c * Q : (c + 1) * Q] = piece.astype(F32)
         before = before + run[:, Q - 1 : Q]
-    fill_pick(pick, flag_ref)
     log_pieces = cums[...].astype(BF16)
-    per = picked_ref.shape[1]
-    step = min(per, Q)
+    gate_ref = gate()
+    out_map_ref = out_map()
+    res_ref = res()
     for g in range(pick.shape[0] // Q):
         these = slice(g * Q, (g + 1) * Q)
         chosen = pick[these]
-        gate = dot(chosen, gate_ref[...], NT)
-        silu_ref[these] = gate / (1.0 + jnp.exp(-gate))
+        at = dot(chosen, gate_ref[...], NT)
+        silu_out.ref[these] = at / (1.0 + jnp.exp(-at))
         logs_at = dot(chosen, log_pieces, NT)
         for h in range(heads):
             run = logs_at[:, h : h + 1] + logs_at[:, 8 + h : 9 + h] + logs_at[:, 16 + h : 17 + h]
-            factor_ref[these, h * width : (h + 1) * width] = jnp.broadcast_to(
+            factor_out.ref[these, h * width : (h + 1) * width] = jnp.broadcast_to(
                 jnp.exp(run), (Q, width)
             )
-        rows_ref[these] = dot(chosen, out_map_ref[...]).astype(BF16)
-        taken = dot(chosen, res_ref[...], NT).astype(BF16)
-        for j in range(0, Q, step):
-            to, at = divmod(g * Q + j, per)
-            picked_ref[to, at : at + step] = taken[j : j + step]
+        rows_out.ref[these] = dot(chosen, out_map_ref[...]).astype(BF16)
+        picked_out.ref[these] = dot(chosen, res_ref[...], NT).astype(BF16)
+        for out in (silu_out, factor_out, rows_out, picked_out):
+            out.send(these)
 
 
 def ssd_kernel(
     heads,
     skip_ref,
-    x_ref,
-    in_ref,
-    out_map_ref,
-    step_ref,
-    decay_ref,
-    flag_ref,
-    value_ref,
+    x,
+    in_map,
+    out_map,
+    step,
+    decay,
+    flags,
+    value_out,
     y_all,
     scaled,
     state,
     pick,
 ):
-    width = x_ref.shape[0] // heads
+    width = x.shape[0] // heads
+    flag_ref = flags()
     chunks = flag_ref.shape[0]
+    fill_pick(pick, flag_ref)
     row = lax.broadcasted_iota(jnp.int32, (Q, Q), 0)
     col = lax.broadcasted_iota(jnp.int32, (Q, Q), 1)
     mask = row <= col
-    logs = chunk_rows(decay_ref, heads)
+    logs = chunk_rows(decay(), heads)
     run_row = dot3(logs, below((Q, Q)))
     run_col = dot3r(jnp.where(col <= row, 1.0, 0.0).astype(BF16), logs)
     state[...] = jnp.zeros_like(state)
+    step_ref = step()
+    in_ref = in_map()
+    out_map_ref = out_map()
+    x_ref = x()
     for c in range(chunks):
         lanes = slice(c * Q, (c + 1) * Q)
         b = in_ref[lanes, :]
@@ -236,68 +245,119 @@
             state[part] = state[part] * jnp.exp(last)
         if c < chunks - 1:
             state[...] += dot(scaled[...], b)
-    fill_pick(pick, flag_ref)
     for g in range(pick.shape[0] // Q):
         these = slice(g * Q, (g + 1) * Q)
-        value_ref[these] = dot(pick[these], y_all[...], NT)
-
-
-def gate_kernel(heads, in_ref, rows_ref, value_ref, factor_ref, silu_ref, gain_ref, out_ref):
+        value_out.ref[these] = dot(pick[these], y_all[...], NT)
+        value_out.send(these)
+
+
+def gate_kernel(heads, in_ref, rows, value, factor, silu, picked, out_ref):
     parts = in_ref.shape[0]
-    rows = in_ref.shape[1] // heads
+    rows_each = in_ref.shape[1] // heads
     per = out_ref.shape[1]
-    columns = value_ref.shape[1]
+    columns = value.shape[1]
     held = in_ref[...].astype(F32)
-    states = [held[:, h * rows : (h + 1) * rows].reshape(parts * rows, Q) for h in range(heads)]
+    states = [
+        held[:, h * rows_each : (h + 1) * rows_each].reshape(parts * rows_each, Q)
+        for h in range(heads)
+    ]
     incoming = jnp.concatenate(states, axis=0).astype(BF16)
-    outer = dot(rows_ref[...], incoming, NT)
-    gated = (value_ref[...] + factor_ref[...] * outer) * silu_ref[...]
-    squares = jnp.sum(gated * gated, axis=1, keepdims=True)
-    scaled = (gated * gain_ref[...].astype(F32)).astype(BF16)
-    slots = gated.shape[0]
-    pad = out_ref.shape[2] - columns
-    lane = lax.broadcasted_iota(jnp.int32, (slots, pad), 1)
-    hi, mid, low = pieces(jnp.broadcast_to(squares, (slots, pad)))
-    extra = jnp.where(
-        lane == 0,
-        hi.astype(F32),
-        jnp.where(lane == 1, mid.astype(F32), jnp.where(lane == 2, low.astype(F32), 0.0)),
-    ).astype(BF16)
-    for j in range(slots // per):
+    outer = dot(rows()[...], incoming, NT)
+    gated = ((value()[...] + factor()[...] * outer) * silu()[...]).astype(BF16)
+    kept = picked()[...]
+    for j in range(out_ref.shape[0]):
         these = slice(j * per, (j + 1) * per)
-        out_ref[j, :, :columns] = scaled[these]
-        out_ref[j, :, columns:] = extra[these]
-
-
-def project_kernel(full_width, in_ref, res_ref, weight_ref, out_ref, lhs, res):
-    groups, per, _ = in_ref.shape
-    columns = res_ref.shape[2]
-    halves = weight_ref.shape[0]
-    half = weight_ref.shape[2]
+        out_ref[j, :, :columns] = gated[these]
+        out_ref[j, :, columns:] = kept[these]
+
+
+def project_kernel(full_width, in_ref, weight, out_ref, lhs, res):
+    groups, per, columns = in_ref.shape
+    columns = columns // 2
     squares = jnp.zeros((per, 1), F32)
     for z in range(groups):
         block = in_ref[z]
-        lhs[:, z * columns : (z + 1) * columns] = block[:, :columns]
-        res[:, z * columns : (z + 1) * columns] = res_ref[z]
-        squares = squares + jnp.sum(block[:, columns:].astype(F32), axis=1, keepdims=True)
+        own = block[:, :columns]
+        lhs[:, z * columns : (z + 1) * columns] = own
+        res[:, z * columns : (z + 1) * columns] = block[:, columns:]
+        own = own.astype(F32)
+        squares = squares + jnp.sum(own * own, axis=1, keepdims=True)
     scale = lax.rsqrt(squares / full_width + 1e-05)
+    halves, _, half = weight.shape
     for k in range(halves):
         part = slice(k * half, (k + 1) * half)
-        done = dot(lhs[...], weight_ref[k])
+        done = dot(lhs[...], weight(k)[...])
         out_ref[:, part] = (done * scale + res[:, part].astype(F32)).astype(BF16)
 
 
-def call(kernel, outs, args, scratch=(), smem=0, name=None, mib=4):
-    vmem = pl.BlockSpec(memory_space=pltpu.VMEM)
-    specs = [pl.BlockSpec(memory_space=pltpu.SMEM)] * smem + [vmem] * (len(args) - smem)
+class Source:
+    def __init__(self, hbm, ref, sem, split):
+        self.shape = hbm.shape
+        if split:
+            n = hbm.shape[0]
+            self.parts = [ref.at[k] for k in range(n)]
+            self.copies = [
+                pltpu.make_async_copy(hbm.at[k], ref.at[k], sem.at[k]) for k in range(n)
+            ]
+        else:
+            self.parts = [ref]
+            self.copies = [pltpu.make_async_copy(hbm, ref, sem.at[0])]
+        for copy in self.copies:
+            copy.start()
+
+    def __call__(self, k=0):
+        self.copies[k].wait()
+        return self.parts[k]
+
+
+class Target:
+    def __init__(self, hbm, ref, sem):
+        self.hbm, self.ref, self.sem, self.copies = hbm, ref, sem, []
+
+    def send(self, these):
+        k = len(self.copies)
+        copy = pltpu.make_async_copy(self.ref.at[these], self.hbm.at[these], self.sem.at[k])
+        copy.start()
+        self.copies.append(copy)
+
+
+def call(kernel, outs, args, scratch=(), places="", to="v", name=None, mib=0):
+    spaces = {"v": pltpu.VMEM, "s": pltpu.SMEM, "h": pltpu.HBM, "p": pltpu.HBM}
     many = isinstance(outs, (tuple, list))
+    results = list(outs) if many else [outs]
+    far_in = [i for i, p in enumerate(places) if p in "hp"]
+    far_out = [i for i, p in enumerate(to) if p == "h"]
+    buffers = [pltpu.VMEM(args[i].shape, args[i].dtype) for i in far_in]
+    buffers += [pltpu.VMEM(results[i].shape, results[i].dtype) for i in far_out]
+    sems = [
+        pltpu.SemaphoreType.DMA((args[i].shape[0] if places[i] == "p" else 1,)) for i in far_in
+    ]
+    sems += [pltpu.SemaphoreType.DMA((4,)) for _ in far_out]
+
+    def body(*refs):
+        ins = list(refs[: len(args)])
+        res = list(refs[len(args) : len(args) + len(results)])
+        rest = refs[len(args) + len(results) :]
+        own = rest[: len(scratch)]
+        held = rest[len(scratch) : len(scratch) + len(buffers)]
+        flagged = rest[len(scratch) + len(buffers) :]
+        for k, i in enumerate(far_in):
+            ins[i] = Source(ins[i], held[k], flagged[k], places[i] == "p")
+        for k, i in enumerate(far_out):
+            res[i] = Target(res[i], held[len(far_in) + k], flagged[len(far_in) + k])
+        kernel(*ins, *res, *own)
+        for i in far_out:
+            for copy in res[i].copies:
+                copy.wait()
+
+    out_specs = [pl.BlockSpec(memory_space=spaces[p]) for p in to]
     return pl.pallas_call(
-        kernel,
+        body,
         out_shape=outs,
-        in_specs=specs,
-        out_specs=[vmem] * len(outs) if many else vmem,
-        scratch_shapes=list(scratch),
-        compiler_params=pltpu.CompilerParams(vmem_limit_bytes=mib << 20),
+        in_specs=[pl.BlockSpec(memory_space=spaces[p]) for p in places],
+        out_specs=out_specs if many else out_specs[0],
+        scratch_shapes=[*scratch, *buffers, *sems],
+        compiler_params=pltpu.CompilerParams(vmem_limit_bytes=mib << 20) if mib else None,
         name=name,
     )(*args)
 
@@ -336,12 +396,13 @@
         S((parts, height, Q), BF16),
         (head_input, input_map, step_size, log_decay),
         [pltpu.VMEM((local_width, length), BF16)],
+        places="hhhh",
         name="final_state",
-        mib=8,
     )
     state, flags, out_weight = held((state, flags, out_weight))
     half = full_width // lax.axis_size("core")
     own = lax.dynamic_slice_in_dim(out_weight, lax.axis_index("core") * half, half, 1)
+    own = (own.astype(F32) * norm_gain.astype(F32)[:, None]).astype(BF16)
     weight = lax.all_gather(own[None], ("core", "head"), axis=0, tiled=True)
     weight = weight.reshape(lax.axis_size("core"), shares * local_width, half)
     moved = lax.all_to_all(state, group, 0, 0, tiled=True)
@@ -351,12 +412,13 @@
             S((slots, local_width), F32),
             S((slots, local_width), F32),
             S((slots, Q), BF16),
-            S((shares, per, local_width), BF16),
+            S((slots, local_width), BF16),
         ),
         (gate_input, residual, output_map, log_decay, flags),
         [pltpu.VMEM((24, length), F32), pltpu.VMEM((slots, length), BF16)],
+        places="hhhhh",
+        to="hhhh",
         name="pick",
-        mib=12,
     )
     moved, picked = held((moved, picked))
     before, factor, total = call(
@@ -367,11 +429,13 @@
             S((groups, height, Q), BF16),
         ),
         (moved,),
+        places="v",
+        to="vvv",
         name="group_scan",
-    )
-    total, flags, picked = held((total, flags, picked))
+        mib=2,
+    )
+    total, flags = held((total, flags))
     totals = lax.all_to_all(total, "y", 0, 0, tiled=True)
-    kept = lax.all_to_all(picked, "head", 0, 0, tiled=True)
     value = call(
         functools.partial(ssd_kernel, heads),
         S((slots, local_width), F32),
@@ -382,33 +446,35 @@
             pltpu.VMEM((local_width, Q), F32),
             pltpu.VMEM((slots, length), BF16),
         ],
-        smem=1,
+        places="shhhhhh",
+        to="h",
         name="ssd",
-        mib=12,
     )
     totals, value = held((totals, value))
     incoming = call(
         functools.partial(combine_kernel, heads),
         S((parts, used, Q), BF16),
         (totals, before, factor),
+        places="vvv",
         name="combine",
+        mib=2,
     )
     incoming = lax.all_to_all(incoming, group, 0, 0, tiled=True)
     gated = call(
         functools.partial(gate_kernel, heads),
-        S((shares, per, -(-(local_width + 3) // Q) * Q), BF16),
-        (incoming, rows, value, since, silu, norm_gain.reshape(1, local_width)),
+        S((shares, per, 2 * local_width), BF16),
+        (incoming, rows, value, since, silu, picked),
+        places="vhhhhh",
         name="gated",
-        mib=6,
     )
     gathered = lax.all_to_all(gated, "head", 0, 0, tiled=True)
     return call(
         functools.partial(project_kernel, full_width),
         S((per, full_width), BF16),
-        (gathered, kept, weight),
+        (gathered, weight),
         [pltpu.VMEM((per, full_width), BF16), pltpu.VMEM((per, full_width), BF16)],
+        places="vp",
         name="project",
-        mib=10,
     )
 
 

time: 104 us -> 89.8 us (0.86); the launches traced: 101 us -> 88.5 us
  local copies, waits for them, and re-layouts: 18.8 us -> 0 us
  Pallas kernels: 13.8 us -> 26.1 us
  blocking collectives: 22.6 us -> 33 us
  waiting for transfers between devices: 9.77 us -> 0.02 us
  starting transfers between devices: 23 us -> 13.5 us
  other arithmetic: 0 us -> 2.47 us
    unnamed x56 -> x0, local copies, waits for them, and re-layouts: 18 us -> none
    pallas_call x7, Pallas kernels: 13.8 us -> 26.1 us  [call(): pl.pallas_call(body, out_shape=outs, in_specs=[pl.BlockSpec(memory_space=...]
    all_to_all x1, blocking collectives: 12 us -> 23.2 us  [on_device(): gathered = lax.all_to_all(gated, 'head', 0, 0, tiled=True)]
    all_to_all x1 -> x0, starting transfers between devices: 8.88 us -> none  [on_device(): kept = lax.all_to_all(picked, 'head', 0, 0, tiled=True)]
    all_to_all x1 -> x0, waiting for transfers between devices: 7.93 us -> none  [on_device(): kept = lax.all_to_all(picked, 'head', 0, 0, tiled=True)]
    convert_element_type x0 -> x2, other arithmetic: none -> 2.47 us  [on_device(): own = (own.astype(F32) * norm_gain.astype(F32)[:, None]).astype(BF16)]
    all_to_all x1, waiting for transfers between devices: 1.82 us -> 0.01 us  [on_device(): totals = lax.all_to_all(total, 'y', 0, 0, tiled=True)]
  transfers between devices with their start and end apart: 4 -> 3, of which waited for: 2 -> 0; matrix products, arithmetic and copies ran while one was open for 0% -> 0% of each run, Pallas kernels for 11% -> 21%
where the time goes in v3:
time: 89.8 us; the launch traced here: 88.5 us
  blocking collectives  33 us (37%)
  Pallas kernels  26.1 us (29%)
  starting transfers between devices  13.5 us (15%)
  between operations  13.5 us (15%)
  other arithmetic  2.47 us (3%)
    pallas_call x7, Pallas kernels, call(): pl.pallas_call(body, out_shape=outs, in_specs=[pl.BlockSpec(memory_space=...  26.1 us
    all_to_all x1, blocking collectives, on_device(): gathered = lax.all_to_all(gated, 'head', 0, 0, tiled=True)  23.2 us
    all_to_all x1, starting transfers between devices, on_device(): moved = lax.all_to_all(state, group, 0, 0, tiled=True)  10.1 us
    all_to_all x1, blocking collectives, on_device(): incoming = lax.all_to_all(incoming, group, 0, 0, tiled=True)  9.84 us
    all_to_all x1, starting transfers between devices, on_device(): totals = lax.all_to_all(total, 'y', 0, 0, tiled=True)  3.35 us
    convert_element_type x2, other arithmetic, on_device(): own = (own.astype(F32) * norm_gain.astype(F32)[:, None]).astype(BF16)  2.47 us
  transfers between devices with their start and end apart: 3, of which 0 were waited for; matrix products, arithmetic and copies ran while one was open for 0% of the time, Pallas kernels for 21%

profile of v3, /device:TPU:1, one launch (start us, length us, event | category | flops | bytes accessed | tf_op | source)
XLA Modules:
  0.0 88.5 jit_solution(17864426805756916323)
XLA Ops:
  6.5 0.0 all-gather.3.cloned.1.call-start
  6.5 2.8 %final_state.1 = bf16[8,32,128]{2,1,0:T(8,128)(2,1)} custom-call(bf16[192,2048]{1,0:T(8,128)(2,1)} %refs_1_.5, bf16[2048,128]{1,0:T(8,128)(2,1)} %refs_2_.5, f32[3,2048]{1,0:T(4,128)} %refs_4_.1, f32[3,2048]{1,0:T(4,128)} %refs_5_.1), custom_call_target="tpu_custom_call" | custom-call | tf_op jit(solution)/shard_map/final_state/pallas_call | solution.py:354
  9.3 0.7 convert_element_type.10
  10.0 1.8 %multiply_convert_fusion = bf16[192,768]{1,0:T(8,128)(2,1)} fusion(f32[192]{0:T(256)S(1)} %convert_element_type.10, bf16[192,1536]{1,0:T(8,128)(2,1)} %param.21, s32[]{:T(128)S(6)} %select_n.3), kind=kLoop, calls=%fused_computation | loop fusion | flops 442368 | bytes 590596 | tf_op jit(solution)/shard_map/convert_element_type | solution.py:405
  11.8 0.0 all-gather.3.cloned.1.call-update
  11.8 10.1 %all-to-all-start = ((bf16[8,32,128]{2,1,0:T(8,128)(2,1)}), bf16[8,32,128]{2,1,0:T(8,128)(2,1)S(1)}, u32[]{:S(2)}, u32[]{:S(2)}) async-start(bf16[8,32,128]{2,1,0:T(8,128)(2,1)} %final_state.1), calls=%async_computation | async-start | bytes 131072 | tf_op jit(solution)/shard_map/all_to_all | solution.py:408
  21.9 6.5 %pick.1 = (f32[512,192]{1,0:T(8,128)}, f32[512,192]{1,0:T(8,128)}, bf16[512,128]{1,0:T(8,128)(2,1)}, bf16[512,192]{1,0:T(8,128)(2,1)}) custom-call(bf16[192,2048]{1,0:T(8,128)(2,1)} %refs_0_.4, bf16[192,2048]{1,0:T(8,128)(2,1)} %refs_1_.4, bf16[2048,128]{1,0:T(8,128)(2,1)} %refs_3_.5, f32[3,2048]{1,0:T(4,128)} %refs_5_.1, s32[16,128]{1,0:T(8,128)} %bitcast.3), custom_call_target="tpu_custom_call" | custom-call | tf_op jit(solution)/shard_map/pick/pallas_call | solution.py:354
  28.5 0.0 all-to-all-done.refs_0_
  28.5 0.7 group_scan.1
  29.2 3.4 %all-to-all-start.1 = ((bf16[8,32,128]{2,1,0:T(8,128)(2,1)}), bf16[8,32,128]{2,1,0:T(8,128)(2,1)S(1)}, u32[]{:S(2)}, u32[]{:S(2)}) async-start(bf16[8,32,128]{2,1,0:T(8,128)(2,1)} %get-tuple-element.26), calls=%async_computation.1 | async-start | bytes 131072 | tf_op jit(solution)/shard_map/all_to_all | solution.py:438
  32.6 7.9 %ssd.1.refs_2_ = f32[512,192]{1,0:T(8,128)} custom-call(f32[3]{0:T(128)} %refs_0_.5, bf16[192,2048]{1,0:T(8,128)(2,1)} %refs_1_.5, bf16[2048,128]{1,0:T(8,128)(2,1)} %refs_2_.5, bf16[2048,128]{1,0:T(8,128)(2,1)} %refs_3_.5, f32[3,2048]{1,0:T(4,128)} %refs_4_.1, f32[3,2048]{1,0:T(4,128)} %refs_5_.1, s32[16,128]{1,0:T(8,128)} %bitcast.4), custom_call_target="tpu_custom_call" | custom-call | tf_op jit(solution)/shard_map/ssd/pallas_call | solution.py:354
  40.5 0.0 all-to-all-done.1.refs_0_
  40.6 0.1 combine.1
  40.7 9.8 %all_to_all.20.refs_0_ = bf16[8,24,128]{2,1,0:T(8,128)(2,1)} all-to-all(bf16[8,24,128]{2,1,0:T(8,128)(2,1)S(1)} %combine.1), channel_id=1, replica_groups=mesh['y'=8,'x'=4,'core'=2,'head'=8] {'x','core'}, dimensions={0} | all-to-all | bytes 98304 | tf_op jit(solution)/shard_map/all_to_all | solution.py:462
  50.5 3.2 %gated.1 = bf16[8,64,384]{2,1,0:T(8,128)(2,1)} custom-call(bf16[8,24,128]{2,1,0:T(8,128)(2,1)} %all_to_all.20.refs_0_, bf16[512,128]{1,0:T(8,128)(2,1)} %get-tuple-element.31.refs_1_, f32[512,192]{1,0:T(8,128)} %ssd.1.refs_2_, f32[512,192]{1,0:T(8,128)} %get-tuple-element.33.refs_3_, f32[512,192]{1,0:T(8,128)} %get-tuple-element.34.refs_4_, ...), custom_call_target="tpu_custom_call" | custom-call | tf_op jit(solution)/shard_map/gated/pallas_call | solution.py:354
  53.8 23.2 %all_to_all.21.refs_0_ = bf16[8,64,384]{2,1,0:T(8,128)(2,1)} all-to-all(bf16[8,64,384]{2,1,0:T(8,128)(2,1)} %gated.1), channel_id=1, replica_groups=mesh['y'=8,'x'=4,'core'=2,'head'=8] {'head'}, dimensions={0} | all-to-all | bytes 786432 | tf_op jit(solution)/shard_map/all_to_all | solution.py:470
  76.9 0.0 all-gather.3.cloned.1.call-done
  76.9 4.7 %project.1 = bf16[64,1536]{1,0:T(8,128)(2,1)} custom-call(bf16[8,64,384]{2,1,0:T(8,128)(2,1)} %all_to_all.21.refs_0_, bf16[2,1536,768]{2,1,0:T(8,128)(2,1)} %bitcast.2), custom_call_target="tpu_custom_call" | custom-call | tf_op jit(solution)/shard_map/project/pallas_call | solution.py:354
Async XLA Ops:
  6.5 70.4 %all-gather.3.cloned.1.call-start = ((), (), s32[]{:S(2)}) async-start(), calls=%async_computation.4 | async-start | bytes 5013504 | tf_op jit(solution)/shard_map/all_gather | solution.py:406
  11.8 16.7 %all-to-all-start = ((bf16[8,32,128]{2,1,0:T(8,128)(2,1)}), bf16[8,32,128]{2,1,0:T(8,128)(2,1)S(1)}, u32[]{:S(2)}, u32[]{:S(2)}) async-start(bf16[8,32,128]{2,1,0:T(8,128)(2,1)} %final_state.1), calls=%async_computation | async-start | bytes 131072 | tf_op jit(solution)/shard_map/all_to_all | solution.py:408
  29.2 11.3 %all-to-all-start.1 = ((bf16[8,32,128]{2,1,0:T(8,128)(2,1)}), bf16[8,32,128]{2,1,0:T(8,128)(2,1)S(1)}, u32[]{:S(2)}, u32[]{:S(2)}) async-start(bf16[8,32,128]{2,1,0:T(8,128)(2,1)} %get-tuple-element.26), calls=%async_computation.1 | async-start | bytes 131072 | tf_op jit(solution)/shard_map/all_to_all | solution.py:438
Sparse Core Ops, SparseCore 0:
  12.0 51.4 all-gather.2

commit v4 on v3

--- a/solution.py
+++ b/solution.py
@@ -58,7 +58,13 @@
     return jnp.concatenate([tile, jnp.zeros((rows - heads, Q), F32)], axis=0)
 
 
-def final_state_kernel(heads, parts, x, in_map, step, decay, out_ref, scaled):
+def final_state_kernel(
+    heads, parts, gain_ref, weight_hbm, x, in_map, step, decay, out_ref, weight_out, scaled, taken, sem
+):
+    half = taken.shape[1]
+    first = pl.multiple_of(lax.axis_index("core") * half, Q)
+    fetch = pltpu.make_async_copy(weight_hbm.at[:, pl.ds(first, half)], taken, sem)
+    fetch.start()
     width = x.shape[0] // heads
     length = x.shape[1]
     chunks = length // Q
@@ -69,6 +75,16 @@
     )
     suffix = dot3(logs, jnp.where(after, 1.0, 0.0).astype(BF16))
     sums = jnp.sum(logs, axis=1, keepdims=True)
+    local = taken.shape[0]
+    same = lax.broadcasted_iota(jnp.int32, (local, local), 0) == lax.broadcasted_iota(
+        jnp.int32, (local, local), 1
+    )
+    gain = jnp.sum(jnp.where(same, gain_ref[...].astype(F32), 0.0), axis=1, keepdims=True)
+    fetch.wait()
+    for k in range(4):
+        rows_k = slice(k * (local // 4), (k + 1) * (local // 4))
+        weight_out.ref[rows_k] = (taken[rows_k].astype(F32) * gain[rows_k]).astype(BF16)
+        weight_out.send(rows_k)
     later = jnp.zeros((heads, 1), F32)
     step_ref = step()
     x_ref = x()
@@ -148,21 +164,8 @@
             pick[g * Q : (g + 1) * Q, c * Q : (c + 1) * Q] = jnp.where(hit, 1.0, 0.0).astype(BF16)
 
 
-def pick_kernel(
-    heads,
-    gate,
-    res,
-    out_map,
-    decay,
-    flags,
-    silu_out,
-    factor_out,
-    rows_out,
-    picked_out,
-    cums,
-    pick,
-):
-    width = gate.shape[0] // heads
+def pick_kernel(heads, gate, res, out_map, decay, flags, picked_out, factor_out, cums, pick):
+    local = gate.shape[0]
     flag_ref = flags()
     chunks = flag_ref.shape[0]
     fill_pick(pick, flag_ref)
@@ -173,25 +176,16 @@
         for i, piece in enumerate(pieces(run + before)):
             cums[i * 8 : i * 8 + heads, c * Q : (c + 1) * Q] = piece.astype(F32)
         before = before + run[:, Q - 1 : Q]
-    log_pieces = cums[...].astype(BF16)
-    gate_ref = gate()
-    out_map_ref = out_map()
-    res_ref = res()
-    for g in range(pick.shape[0] // Q):
-        these = slice(g * Q, (g + 1) * Q)
-        chosen = pick[these]
-        at = dot(chosen, gate_ref[...], NT)
-        silu_out.ref[these] = at / (1.0 + jnp.exp(-at))
-        logs_at = dot(chosen, log_pieces, NT)
-        for h in range(heads):
-            run = logs_at[:, h : h + 1] + logs_at[:, 8 + h : 9 + h] + logs_at[:, 16 + h : 17 + h]
-            factor_out.ref[these, h * width : (h + 1) * width] = jnp.broadcast_to(
-                jnp.exp(run), (Q, width)
-            )
-        rows_out.ref[these] = dot(chosen, out_map_ref[...]).astype(BF16)
-        picked_out.ref[these] = dot(chosen, res_ref[...], NT).astype(BF16)
-        for out in (silu_out, factor_out, rows_out, picked_out):
-            out.send(these)
+    chosen = pick[...]
+    logs = dot(chosen, cums[...].astype(BF16), NT)
+    logs = logs[:, 0:heads] + logs[:, 8 : 8 + heads] + logs[:, 16 : 16 + heads]
+    factor_out.ref[:, 0:heads] = jnp.exp(logs)
+    factor_out.send(slice(None))
+    ref = picked_out.ref
+    ref[:, :local] = dot(chosen, gate()[...], NT).astype(BF16)
+    ref[:, local : 2 * local] = dot(chosen, res()[...], NT).astype(BF16)
+    ref[:, 2 * local :] = dot(chosen, out_map()[...]).astype(BF16)
+    picked_out.send(slice(None))
 
 
 def ssd_kernel(
@@ -245,33 +239,39 @@
             state[part] = state[part] * jnp.exp(last)
         if c < chunks - 1:
             state[...] += dot(scaled[...], b)
-    for g in range(pick.shape[0] // Q):
-        these = slice(g * Q, (g + 1) * Q)
-        value_out.ref[these] = dot(pick[these], y_all[...], NT)
-        value_out.send(these)
-
-
-def gate_kernel(heads, in_ref, rows, value, factor, silu, picked, out_ref):
+    value_out.ref[...] = dot(pick[...], y_all[...], NT).astype(BF16)
+    value_out.send(slice(None))
+
+
+def gate_kernel(heads, in_ref, picked, factor, value, out_ref):
     parts = in_ref.shape[0]
     rows_each = in_ref.shape[1] // heads
     per = out_ref.shape[1]
     columns = value.shape[1]
+    width = columns // heads
     held = in_ref[...].astype(F32)
     states = [
         held[:, h * rows_each : (h + 1) * rows_each].reshape(parts * rows_each, Q)
         for h in range(heads)
     ]
     incoming = jnp.concatenate(states, axis=0).astype(BF16)
-    outer = dot(rows()[...], incoming, NT)
-    gated = ((value()[...] + factor()[...] * outer) * silu()[...]).astype(BF16)
-    kept = picked()[...]
+    picked_ref = picked()
+    outer = dot(picked_ref[:, 2 * columns :], incoming, NT)
+    factor_ref = factor()
+    value_ref = value()
     for j in range(out_ref.shape[0]):
         these = slice(j * per, (j + 1) * per)
-        out_ref[j, :, :columns] = gated[these]
-        out_ref[j, :, columns:] = kept[these]
-
-
-def project_kernel(full_width, in_ref, weight, out_ref, lhs, res):
+        since = jnp.concatenate(
+            [jnp.broadcast_to(factor_ref[these, h : h + 1], (per, width)) for h in range(heads)],
+            axis=1,
+        )
+        gate = picked_ref[these, :columns].astype(F32)
+        y = value_ref[these].astype(F32) + since * outer[these]
+        out_ref[j, :, :columns] = (y * (gate / (1.0 + jnp.exp(-gate)))).astype(BF16)
+        out_ref[j, :, columns:] = picked_ref[these, columns : 2 * columns]
+
+
+def project_kernel(full_width, in_ref, mine, other, out_ref, lhs, res):
     groups, per, columns = in_ref.shape
     columns = columns // 2
     squares = jnp.zeros((per, 1), F32)
@@ -283,21 +283,25 @@
         own = own.astype(F32)
         squares = squares + jnp.sum(own * own, axis=1, keepdims=True)
     scale = lax.rsqrt(squares / full_width + 1e-05)
-    halves, _, half = weight.shape
-    for k in range(halves):
-        part = slice(k * half, (k + 1) * half)
-        done = dot(lhs[...], weight(k)[...])
-        out_ref[:, part] = (done * scale + res[:, part].astype(F32)).astype(BF16)
+    half = mine.shape[1]
+    core = lax.axis_index("core")
+    for weight, at in ((mine, core), (other, 1 - core)):
+        step = half // 2
+        for k in range(2):
+            columns_k = pl.ds(pl.multiple_of(at * half + k * step, Q), step)
+            done = dot(lhs[...], weight[:, k * step : (k + 1) * step])
+            out_ref[:, columns_k] = (done * scale + res[:, columns_k].astype(F32)).astype(BF16)
 
 
 class Source:
     def __init__(self, hbm, ref, sem, split):
         self.shape = hbm.shape
         if split:
-            n = hbm.shape[0]
-            self.parts = [ref.at[k] for k in range(n)]
+            step = hbm.shape[1] // 2
+            parts = [(slice(None), slice(k * step, (k + 1) * step)) for k in range(2)]
+            self.parts = [ref.at[p] for p in parts]
             self.copies = [
-                pltpu.make_async_copy(hbm.at[k], ref.at[k], sem.at[k]) for k in range(n)
+                pltpu.make_async_copy(hbm.at[p], ref.at[p], sem.at[k]) for k, p in enumerate(parts)
             ]
         else:
             self.parts = [ref]
@@ -322,7 +326,7 @@
 
 
 def call(kernel, outs, args, scratch=(), places="", to="v", name=None, mib=0):
-    spaces = {"v": pltpu.VMEM, "s": pltpu.SMEM, "h": pltpu.HBM, "p": pltpu.HBM}
+    spaces = {"v": pltpu.VMEM, "s": pltpu.SMEM, "h": pltpu.HBM, "p": pltpu.HBM, "r": pltpu.HBM}
     many = isinstance(outs, (tuple, list))
     results = list(outs) if many else [outs]
     far_in = [i for i, p in enumerate(places) if p in "hp"]
@@ -330,7 +334,7 @@
     buffers = [pltpu.VMEM(args[i].shape, args[i].dtype) for i in far_in]
     buffers += [pltpu.VMEM(results[i].shape, results[i].dtype) for i in far_out]
     sems = [
-        pltpu.SemaphoreType.DMA((args[i].shape[0] if places[i] == "p" else 1,)) for i in far_in
+        pltpu.SemaphoreType.DMA((2,)) for i in far_in
     ]
     sems += [pltpu.SemaphoreType.DMA((4,)) for _ in far_out]
 
@@ -391,33 +395,37 @@
     held = lax.optimization_barrier
     flags = boundary.reshape(length // Q, Q)
 
-    state = call(
+    half = full_width // lax.axis_size("core")
+    state, scaled = call(
         functools.partial(final_state_kernel, heads, parts),
-        S((parts, height, Q), BF16),
-        (head_input, input_map, step_size, log_decay),
-        [pltpu.VMEM((local_width, length), BF16)],
-        places="hhhh",
+        (S((parts, height, Q), BF16), S((local_width, half), BF16)),
+        (
+            norm_gain.reshape(1, local_width),
+            out_weight,
+            head_input,
+            input_map,
+            step_size,
+            log_decay,
+        ),
+        [
+            pltpu.VMEM((local_width, length), BF16),
+            pltpu.VMEM((local_width, half), BF16),
+            pltpu.SemaphoreType.DMA,
+        ],
+        places="vrhhhh",
+        to="vh",
         name="final_state",
     )
-    state, flags, out_weight = held((state, flags, out_weight))
-    half = full_width // lax.axis_size("core")
-    own = lax.dynamic_slice_in_dim(out_weight, lax.axis_index("core") * half, half, 1)
-    own = (own.astype(F32) * norm_gain.astype(F32)[:, None]).astype(BF16)
-    weight = lax.all_gather(own[None], ("core", "head"), axis=0, tiled=True)
-    weight = weight.reshape(lax.axis_size("core"), shares * local_width, half)
+    state, flags = held((state, flags))
+    mine = lax.all_gather(scaled, "head", axis=0, tiled=True)
     moved = lax.all_to_all(state, group, 0, 0, tiled=True)
-    silu, since, rows, picked = call(
+    picked, since = call(
         functools.partial(pick_kernel, heads),
-        (
-            S((slots, local_width), F32),
-            S((slots, local_width), F32),
-            S((slots, Q), BF16),
-            S((slots, local_width), BF16),
-        ),
+        (S((slots, 2 * local_width + Q), BF16), S((slots, Q), F32)),
         (gate_input, residual, output_map, log_decay, flags),
         [pltpu.VMEM((24, length), F32), pltpu.VMEM((slots, length), BF16)],
         places="hhhhh",
-        to="hhhh",
+        to="hh",
         name="pick",
     )
     moved, picked = held((moved, picked))
@@ -438,7 +446,7 @@
     totals = lax.all_to_all(total, "y", 0, 0, tiled=True)
     value = call(
         functools.partial(ssd_kernel, heads),
-        S((slots, local_width), F32),
+        S((slots, local_width), BF16),
         (skip_gain, head_input, input_map, output_map, step_size, log_decay, flags),
         [
             pltpu.VMEM((local_width, length), BF16),
@@ -463,18 +471,22 @@
     gated = call(
         functools.partial(gate_kernel, heads),
         S((shares, per, 2 * local_width), BF16),
-        (incoming, rows, value, since, silu, picked),
-        places="vhhhhh",
+        (incoming, picked, since, value),
+        places="vhhh",
         name="gated",
     )
+    gated, mine = held((gated, mine))
+    cores = lax.axis_size("core")
+    other = lax.ppermute(mine, "core", [(c, cores - 1 - c) for c in range(cores)])
     gathered = lax.all_to_all(gated, "head", 0, 0, tiled=True)
     return call(
         functools.partial(project_kernel, full_width),
         S((per, full_width), BF16),
-        (gathered, weight),
+        (gathered, mine, other),
         [pltpu.VMEM((per, full_width), BF16), pltpu.VMEM((per, full_width), BF16)],
-        places="vp",
+        places="vvv",
         name="project",
+        mib=8,
     )
 
 

time: 89.8 us -> 94.3 us (1.050)
  starting transfers between devices: 13.5 us -> 19.7 us
  blocking collectives: 33 us -> 29.6 us
  local copies, waits for them, and re-layouts: 0 us -> 2.9 us
  other arithmetic: 2.47 us -> 0 us
  waiting for transfers between devices: 0.02 us -> 2.44 us
    ppermute x0 -> x1, starting transfers between devices: none -> 6.28 us  [on_device(): lax.ppermute(mine, 'core', [(c, cores - 1 - c) for c in range(cores)])]
    all_to_all x1, blocking collectives: 23.2 us -> 19.5 us  [on_device(): gathered = lax.all_to_all(gated, 'head', 0, 0, tiled=True)]
    convert_element_type x2 -> x0, other arithmetic: 2.47 us -> none  [on_device(): own = (own.astype(F32) * norm_gain.astype(F32)[:, None]).astype(BF16)]
    all_gather x1, waiting for transfers between devices: 0.01 us -> 2.42 us  [on_device(): mine = lax.all_gather(scaled, 'head', axis=0, tiled=True)]
    unnamed x0 -> x2, local copies, waits for them, and re-layouts: none -> 1.67 us
    reshape x0 -> x1, local copies, waits for them, and re-layouts: none -> 1.23 us  [on_device(): norm_gain.reshape(1, local_width)]
  transfers between devices with their start and end apart: 3 -> 4, of which waited for: 0 -> 1; matrix products, arithmetic and copies ran while one was open for 0% -> 0% of each run, Pallas kernels for 21% -> 22%
where the time goes in v4:
time: 94.3 us; the launch traced here: 93.6 us
  blocking collectives  29.6 us (31%)
  Pallas kernels  25.5 us (27%)
  starting transfers between devices  19.7 us (21%)
  between operations  13.5 us (14%)
  local copies, waits for them, and re-layouts  2.9 us (3%)
  waiting for transfers between devices  2.44 us (3%)
    pallas_call x7, Pallas kernels, call(): pl.pallas_call(body, out_shape=outs, in_specs=[pl.BlockSpec(memory_space=...  25.5 us
    all_to_all x1, blocking collectives, on_device(): gathered = lax.all_to_all(gated, 'head', 0, 0, tiled=True)  19.5 us
    all_to_all x1, starting transfers between devices, on_device(): moved = lax.all_to_all(state, group, 0, 0, tiled=True)  10.1 us
    all_to_all x1, blocking collectives, on_device(): incoming = lax.all_to_all(incoming, group, 0, 0, tiled=True)  10.1 us
    ppermute x1, starting transfers between devices, on_device(): lax.ppermute(mine, 'core', [(c, cores - 1 - c) for c in range(cores)])  6.28 us
    all_to_all x1, starting transfers between devices, on_device(): totals = lax.all_to_all(total, 'y', 0, 0, tiled=True)  3.35 us
    all_gather x1, waiting for transfers between devices, on_device(): mine = lax.all_gather(scaled, 'head', axis=0, tiled=True)  2.42 us
  transfers between devices with their start and end apart: 4, of which 1 were waited for; matrix products, arithmetic and copies ran while one was open for 0% of the time, Pallas kernels for 22%

profile of v4, /device:TPU:1, one launch (start us, length us, event | category | flops | bytes accessed | tf_op | source)
XLA Modules:
  0.0 93.6 jit_solution(13101419868891120979)
XLA Ops:
  6.5 0.0 all-gather.2.cloned.1.call-start
  6.5 1.2 %reshape.6.refs_0_ = bf16[1,192]{1,0:T(2,128)(2,1)} reshape(bf16[192]{0:T(256)(128)(2,1)} %param.20) | data formatting | bytes 768 | tf_op jit(solution)/shard_map/reshape | solution.py:403
  7.8 3.6 %final_state.1 = (bf16[8,32,128]{2,1,0:T(8,128)(2,1)}, bf16[192,768]{1,0:T(8,128)(2,1)}) custom-call(bf16[1,192]{1,0:T(2,128)(2,1)} %reshape.6.refs_0_, bf16[192,1536]{1,0:T(8,128)(2,1)} %refs_1_.3, bf16[192,2048]{1,0:T(8,128)(2,1)} %refs_1_.5, bf16[2048,128]{1,0:T(8,128)(2,1)} %refs_2_.5, f32[3,2048]{1,0:T(4,128)} %refs_4_.3, f32[3,2048]{1,0:T(4,128)} %refs_5_.3), custom_call_target="tpu_custom_call" | custom-call | tf_op jit(solution)/shard_map/final_state/pallas_call | solution.py:358
  11.4 0.0 all-gather.2.cloned.1.call-update
  11.4 10.1 %all-to-all-start = ((bf16[8,32,128]{2,1,0:T(8,128)(2,1)}), bf16[8,32,128]{2,1,0:T(8,128)(2,1)S(1)}, u32[]{:S(2)}, u32[]{:S(2)}) async-start(bf16[8,32,128]{2,1,0:T(8,128)(2,1)} %get-tuple-element.23), calls=%async_computation | async-start | bytes 131072 | tf_op jit(solution)/shard_map/all_to_all | solution.py:421
  21.5 8.5 %pick.1 = (bf16[512,512]{1,0:T(8,128)(2,1)}, f32[512,128]{1,0:T(8,128)}) custom-call(bf16[192,2048]{1,0:T(8,128)(2,1)} %refs_0_.2, bf16[192,2048]{1,0:T(8,128)(2,1)} %refs_1_.4, bf16[2048,128]{1,0:T(8,128)(2,1)} %refs_3_.5, f32[3,2048]{1,0:T(4,128)} %refs_5_.3, s32[16,128]{1,0:T(8,128)} %bitcast.1), custom_call_target="tpu_custom_call" | custom-call | tf_op jit(solution)/shard_map/pick/pallas_call | solution.py:358
  30.1 0.0 all-to-all-done.refs_0_
  30.1 0.7 group_scan.1
  30.8 3.4 %all-to-all-start.1 = ((bf16[8,32,128]{2,1,0:T(8,128)(2,1)}), bf16[8,32,128]{2,1,0:T(8,128)(2,1)S(1)}, u32[]{:S(2)}, u32[]{:S(2)}) async-start(bf16[8,32,128]{2,1,0:T(8,128)(2,1)} %get-tuple-element.28), calls=%async_computation.1 | async-start | bytes 131072 | tf_op jit(solution)/shard_map/all_to_all | solution.py:446
  34.2 7.7 %ssd.1.refs_3_ = bf16[512,192]{1,0:T(8,128)(2,1)} custom-call(f32[3]{0:T(128)} %refs_0_.3, bf16[192,2048]{1,0:T(8,128)(2,1)} %refs_1_.5, bf16[2048,128]{1,0:T(8,128)(2,1)} %refs_2_.5, bf16[2048,128]{1,0:T(8,128)(2,1)} %refs_3_.5, f32[3,2048]{1,0:T(4,128)} %refs_4_.3, f32[3,2048]{1,0:T(4,128)} %refs_5_.3, s32[16,128]{1,0:T(8,128)} %bitcast.2), custom_call_target="tpu_custom_call" | custom-call | tf_op jit(solution)/shard_map/ssd/pallas_call | solution.py:358
  41.9 0.0 all-to-all-done.1.refs_0_
  41.9 0.1 combine.1
  42.0 10.1 %all_to_all.20.refs_0_ = bf16[8,24,128]{2,1,0:T(8,128)(2,1)} all-to-all(bf16[8,24,128]{2,1,0:T(8,128)(2,1)S(1)} %combine.1), channel_id=1, replica_groups=mesh['y'=8,'x'=4,'core'=2,'head'=8] {'x','core'}, dimensions={0} | all-to-all | bytes 98304 | tf_op jit(solution)/shard_map/all_to_all | solution.py:470
  52.1 3.2 %gated.1 = bf16[8,64,384]{2,1,0:T(8,128)(2,1)} custom-call(bf16[8,24,128]{2,1,0:T(8,128)(2,1)} %all_to_all.20.refs_0_, bf16[512,512]{1,0:T(8,128)(2,1)} %get-tuple-element.33.refs_1_, f32[512,128]{1,0:T(8,128)} %get-tuple-element.34.refs_2_, bf16[512,192]{1,0:T(8,128)(2,1)} %ssd.1.refs_3_), custom_call_target="tpu_custom_call" | custom-call | tf_op jit(solution)/shard_map/gated/pallas_call | solution.py:358
  55.3 2.4 %all-gather.2.cloned.1.call-done.refs_1_ = bf16[1536,768]{1,0:T(8,128)(2,1)} async-done(((bf16[192,768]{1,0:T(8,128)(2,1)}), bf16[1536,768]{1,0:T(8,128)(2,1)}) %all-gather.2.cloned.1.call-update) | async-done | bytes 2359312 | tf_op jit(solution)/shard_map/all_gather | solution.py:420
  57.7 6.3 %collective-permute-start = (bf16[1536,768]{1,0:T(8,128)(2,1)}, bf16[1536,768]{1,0:T(8,128)(2,1)S(1)}, u32[]{:S(2)}, u32[]{:S(2)}) collective-permute-start(bf16[1536,768]{1,0:T(8,128)(2,1)} %all-gather.2.cloned.1.call-done.refs_1_), channel_id=1, source_target_pairs={{0,8},{8,0},{1,9},{9,1},{2,10},{10,2},{3,11},{11,3},{4,12},{12,4},... | collective-permute-start | bytes 7077896 | tf_op jit(solution)/shard_map/ppermute | solution.py:480
  64.0 19.5 %all_to_all.21.refs_0_ = bf16[8,64,384]{2,1,0:T(8,128)(2,1)S(1)} all-to-all(bf16[8,64,384]{2,1,0:T(8,128)(2,1)} %gated.1), channel_id=1, replica_groups=mesh['y'=8,'x'=4,'core'=2,'head'=8] {'head'}, dimensions={0} | all-to-all | bytes 786432 | tf_op jit(solution)/shard_map/all_to_all | solution.py:481
  83.6 0.0 collective-permute-done.refs_2_
  83.6 0.0 copy-start
  83.6 1.7 %copy-done = bf16[1536,768]{1,0:T(8,128)(2,1)S(1)} copy-done((bf16[1536,768]{1,0:T(8,128)(2,1)S(1)}, bf16[1536,768]{1,0:T(8,128)(2,1)}, u32[]{:S(2)}) %copy-start) | copy-done | bytes 2359320
  85.2 1.6 %project.1 = bf16[64,1536]{1,0:T(8,128)(2,1)} custom-call(bf16[8,64,384]{2,1,0:T(8,128)(2,1)S(1)} %all_to_all.21.refs_0_, bf16[1536,768]{1,0:T(8,128)(2,1)S(1)} %copy-done, bf16[1536,768]{1,0:T(8,128)(2,1)S(1)} %collective-permute-done.refs_2_), custom_call_target="tpu_custom_call" | custom-call | tf_op jit(solution)/shard_map/project/pallas_call | solution.py:358
Async XLA Ops:
  6.5 51.2 %all-gather.2.cloned.1.call-start = ((), (), s32[]{:S(2)}) async-start(), calls=%async_computation.4 | async-start | bytes 2654208 | tf_op jit(solution)/shard_map/all_gather | solution.py:420
  11.4 18.6 %all-to-all-start = ((bf16[8,32,128]{2,1,0:T(8,128)(2,1)}), bf16[8,32,128]{2,1,0:T(8,128)(2,1)S(1)}, u32[]{:S(2)}, u32[]{:S(2)}) async-start(bf16[8,32,128]{2,1,0:T(8,128)(2,1)} %get-tuple-element.23), calls=%async_computation | async-start | bytes 131072 | tf_op jit(solution)/shard_map/all_to_all | solution.py:421
  30.8 11.1 %all-to-all-start.1 = ((bf16[8,32,128]{2,1,0:T(8,128)(2,1)}), bf16[8,32,128]{2,1,0:T(8,128)(2,1)S(1)}, u32[]{:S(2)}, u32[]{:S(2)}) async-start(bf16[8,32,128]{2,1,0:T(8,128)(2,1)} %get-tuple-element.28), calls=%async_computation.1 | async-start | bytes 131072 | tf_op jit(solution)/shard_map/all_to_all | solution.py:446
  57.7 25.8 %collective-permute-start = (bf16[1536,768]{1,0:T(8,128)(2,1)}, bf16[1536,768]{1,0:T(8,128)(2,1)S(1)}, u32[]{:S(2)}, u32[]{:S(2)}) collective-permute-start(bf16[1536,768]{1,0:T(8,128)(2,1)} %all-gather.2.cloned.1.call-done.refs_1_), channel_id=1, source_target_pairs={{0,8},{8,0},{1,9},{9,1},{2,10},{10,2},{3,11},{11,3},{4,12},{12,4},... | collective-permute-start | bytes 7077896 | tf_op jit(solution)/shard_map/ppermute | solution.py:480
  83.6 1.7 %copy-start = (bf16[1536,768]{1,0:T(8,128)(2,1)S(1)}, bf16[1536,768]{1,0:T(8,128)(2,1)}, u32[]{:S(2)}) copy-start(bf16[1536,768]{1,0:T(8,128)(2,1)} %all-gather.2.cloned.1.call-done.refs_1_) | copy-start | bytes 7077892
Sparse Core Ops, SparseCore 0:
  11.5 46.1 all-gather.1
